TPU v7x, 32 devices: a whole 2x2x4 slice. The times are simulated.
32 devices in a mesh: seq: 8 (over z, x), rows: 4 (over y, core).
Axes of the slice: x: 2, y: 2, z: 4, core: 2. Of those that a mesh axis runs over, the one named last changes fastest.
Arguments:
- tokens: bfloat16 [12, 1024, 512], P('rows', 'seq'), may hold values from -6 to 6
- segment_ids: int32 [12, 1024], P('rows', 'seq'), may hold values from 0 to 3, never falling along the last dimension, each value on 1 to 512 neighbouring positions
- padding: int32 [12, 1024], P('rows', 'seq'), may hold values 0 or 1
- gain_one: float32 [512], replicated, may hold values from 0.5 to 1.5
- w_query: bfloat16 [512, 512], replicated, may hold values from -0.25 to 0.25
- w_key: bfloat16 [512, 512], replicated, may hold values from -0.25 to 0.25
- w_value: bfloat16 [512, 512], replicated, may hold values from -0.25 to 0.25
- blend: float32 [2, 8], replicated, may hold values from 0.5 to 2
- w_out: bfloat16 [512, 512], replicated, may hold values from -0.75 to 0.75
- gain_two: float32 [512], replicated, may hold values from 0.5 to 1.5
- w_up: bfloat16 [512, 2048], replicated, may hold values from -0.25 to 0.25
- w_down: bfloat16 [2048, 512], replicated, may hold values from -0.125 to 0.125
- cotangent: bfloat16 [12, 1024, 512], P('rows', 'seq'), may hold values from -6 to 6
Outputs:
- output: bfloat16 [12, 1024, 512], P('rows', 'seq')
- grad_tokens: bfloat16 [12, 1024, 512], P('rows', 'seq')
- grad_gain_one: float32 [512], replicated
- grad_query: float32 [512, 512], replicated
- grad_key: float32 [512, 512], replicated
- grad_value: float32 [512, 512], replicated
- grad_blend: float32 [2, 8], replicated
- grad_out: float32 [512, 512], replicated
- grad_gain_two: float32 [512], replicated
- grad_up: float32 [512, 2048], replicated
- grad_down: float32 [2048, 512], replicated
Inputs may be any that keep to these rules, and one draw needn't show every extreme that they name: `segment_ids`: within a row the ids never fall; each of the 4 documents of a row holds 1 to 512 tokens and one holds exactly 512.
All inputs are finite; a program needn't handle non-finite values. No bound on the sum of `padding` on one device may be relied on, other than what follows from the above.
Results may differ from a plain program's by a relative error of at most 0.014.
Values may be sent and summed in bfloat16 or wider, within the bound.
A program may use at most 256 MiB of HBM per device.

v0:
```python
import math

import jax
import jax.numpy as jnp
from jax import lax
from jax.sharding import PartitionSpec as P

D = 512
H = 8
E = 64
BAND = 30


EPSILON = 1e-06
EXACT_PRECISION = lax.Precision.HIGHEST
NEGATIVE = -1e30


def shifted(block, axis, distance):
    devices = range(lax.axis_size(axis))
    route = [(i - distance, i) for i in devices if i - distance in devices]
    return lax.ppermute(block, axis, route)


def prefix(value, axis, combine, identity):
    count, position = (lax.axis_size(axis), lax.axis_index(axis))
    everything = jax.tree.map(
        lambda part, kind: lax.all_gather(part.astype(kind), axis),
        value,
        (jnp.bfloat16, jnp.bfloat16, jnp.bfloat16, jnp.bfloat16, jnp.bfloat16),
    )
    start = jax.tree.map(
        lambda part, zero: jnp.broadcast_to(jnp.asarray(zero, part.dtype), part.shape),
        value,
        identity,
    )

    def turn(k, before):
        reached = k < position
        new = combine(
            before, jax.tree.map(lambda part, own: part[k].astype(own.dtype), everything, value)
        )
        return jax.tree.map(lambda a, b: jnp.where(reached, a, b), new, before)

    return lax.fori_loop(0, count, turn, start)


def prefix_2(value, axis, join, neutral):
    count = lax.axis_size(axis)
    place = lax.axis_index(axis)
    ahead = count - 1 - place
    gathered = jax.tree.map(
        lambda a, kind: lax.all_gather(a.astype(kind), axis),
        value,
        jax.tree.map(lambda a: jnp.bfloat16 if a.dtype == jnp.float32 else a.dtype, value),
    )
    state = jax.tree.map(lambda a, e: jnp.zeros_like(a) + jnp.asarray(e, a.dtype), value, neutral)

    def one(turn, state):
        source = count - 1 - turn
        return join(
            state,
            jax.tree.map(
                lambda a, own: lax.dynamic_index_in_dim(a, source, 0, False).astype(own.dtype),
                gathered,
                value,
            ),
        )

    return lax.fori_loop(0, ahead, one, state)


def feature_one(values_in):
    return jnp.where(
        values_in > 0, values_in + 1.0, jnp.exp(jnp.where(values_in > 0, 0.0, values_in))
    )


def slope_one(values_in):
    return jnp.where(values_in > 0, 1.0, jnp.exp(jnp.where(values_in > 0, 0.0, values_in)))


def feature_two(values_in):
    return 1.0 + jnp.tanh(values_in)


def slope_two(values_in):
    tangent = jnp.tanh(values_in)
    return 1.0 - tangent * tangent


def norm_apply(inputs, gain_vec):
    inverse = lax.rsqrt(jnp.mean(inputs * inputs, -1, keepdims=True) + EPSILON)
    return (inputs * inverse * gain_vec, inverse)


def norm_back(inputs, inverse, gain_vec, grad_in):
    scaled = grad_in * gain_vec
    return inverse * scaled - inputs * inverse**3 * jnp.mean(inputs * scaled, -1, keepdims=True)


def gelu_value(upward_value):
    return jax.nn.gelu(upward_value, approximate=True)


def join_states(earlier, later):
    later_empty = later[4] < 0.0
    matched = (earlier[4] == later[4]).astype(jnp.float32)

    def grow(older_part, newer_part):
        shape_tail = (-1,) + (1,) * (newer_part.ndim - 1)
        joined = newer_part + matched.reshape(shape_tail) * older_part
        return jnp.where(later_empty.reshape(shape_tail), older_part, joined)

    new_key = jnp.where(later_empty, earlier[4], later[4])
    return (
        grow(earlier[0], later[0]),
        grow(earlier[1], later[1]),
        grow(earlier[2], later[2]),
        grow(earlier[3], later[3]),
        new_key,
    )


def shards(
    tokens,
    segment_ids,
    padding,
    gain_one,
    w_query,
    w_key,
    w_value,
    blend,
    w_out,
    gain_two,
    w_up,
    w_down,
    cotangent,
):
    row_count, tok_count, _ = tokens.shape
    total_rows = row_count * tok_count
    score_scale = 1.0 / math.sqrt(E)
    inputs = tokens.astype(jnp.float32).reshape(total_rows, D)
    normed, inverse_one = norm_apply(inputs, gain_one)
    normed_low = normed.astype(jnp.bfloat16)
    queries = (
        jnp.dot(normed_low, w_query, preferred_element_type=jnp.float32)
        .astype(jnp.bfloat16)
        .reshape(row_count, tok_count, H, E)
    )
    key_rows = (
        jnp.dot(normed_low, w_key, preferred_element_type=jnp.float32)
        .astype(jnp.bfloat16)
        .reshape(row_count, tok_count, H, E)
    )
    value_rows = (
        jnp.dot(normed_low, w_value, preferred_element_type=jnp.float32)
        .astype(jnp.bfloat16)
        .reshape(row_count, tok_count, H, E)
    )
    seg_plus = segment_ids + 1
    key_info = jnp.where(padding == 1, seg_plus, 0)
    tail_from = tok_count - BAND
    halo_keys, neighbor_value_rows, halo_info = shifted(
        (
            key_rows[:, tail_from:],
            value_rows[:, tail_from:],
            key_info[:, tail_from:].astype(jnp.bfloat16),
        ),
        "seq",
        1,
    )
    wide_keys = jnp.concatenate([halo_keys, key_rows], 1)
    wide_values = jnp.concatenate([neighbor_value_rows, value_rows], 1)
    wide_info = jnp.concatenate([halo_info.astype(jnp.float32), key_info.astype(jnp.float32)], 1)
    query_pos = jnp.arange(tok_count)[:, None]
    wide_pos = jnp.arange(tok_count + BAND)[None, :]
    inside = (wide_pos >= query_pos) & (wide_pos <= query_pos + BAND)
    own_key = wide_pos == query_pos + BAND
    near_mask = (
        inside[None]
        & ((wide_info[:, None, :] == seg_plus.astype(jnp.float32)[:, :, None]) | own_key[None])
    )[:, None]

    def near_scores():
        raw_scores = (
            jnp.einsum("rqhe,rkhe->rhqk", queries, wide_keys, preferred_element_type=jnp.float32)
            * score_scale
        )
        return jnp.where(near_mask, raw_scores, NEGATIVE)

    scores = near_scores()
    peak_score = jnp.max(scores, -1, keepdims=True)
    log_total = peak_score + jnp.log(jnp.sum(jnp.exp(scores - peak_score), -1, keepdims=True))
    weights = jnp.exp(scores - log_total)
    near_out = jnp.einsum(
        "rhqk,rkhe->rqhe",
        weights.astype(jnp.bfloat16),
        wide_values,
        preferred_element_type=jnp.float32,
    )
    value_full = value_rows.astype(jnp.float32)
    query_full = queries.astype(jnp.float32)
    key_full = key_rows.astype(jnp.float32)
    local_pos = jnp.arange(tok_count)
    earlier_key = local_pos[None, :] < local_pos[:, None]
    self_key = local_pos[None, :] == local_pos[:, None]
    same_doc = segment_ids[:, :, None] == segment_ids[:, None, :]
    far_mask = (
        same_doc & (earlier_key[None] & (padding[:, None, :] == 1) | self_key[None])
    ).astype(jnp.float32)[:, None]
    far_mask_low = far_mask.astype(jnp.bfloat16)
    last_seg = segment_ids[:, tok_count - 1]
    tail_weight = ((segment_ids == last_seg[:, None]) & (padding == 1)).astype(jnp.float32)

    def far_local(feature):
        feat_q = feature(query_full).astype(jnp.bfloat16)
        feat_k = feature(key_full).astype(jnp.bfloat16)
        kernel = (
            jnp.einsum("rqhe,rkhe->rhqk", feat_q, feat_k, preferred_element_type=jnp.float32)
            * far_mask
        ).astype(jnp.bfloat16)
        numer = jnp.einsum(
            "rhqk,rkhe->rqhe", kernel, value_rows, preferred_element_type=jnp.float32
        )
        denom = jnp.einsum("rhqk->rqh", kernel.astype(jnp.float32))
        weighted_result = feat_k * tail_weight[:, :, None, None].astype(jnp.bfloat16)
        running_state = jnp.einsum(
            "rkhe,rkhf->rhef", weighted_result, value_rows, preferred_element_type=jnp.float32
        )
        norm_state = jnp.sum(weighted_result.astype(jnp.float32), 1)
        return (feat_q, feat_k, kernel, numer, denom, running_state, norm_state)

    local_one = far_local(feature_one)
    local_two = far_local(feature_two)
    key_last = last_seg.astype(jnp.float32)
    empty_state = jnp.zeros_like(local_one[5])
    empty_norm = jnp.zeros_like(local_one[6])
    identity = (
        empty_state,
        empty_norm,
        empty_state,
        empty_norm,
        -jnp.ones((row_count,), jnp.float32),
    )
    incoming = prefix(
        (local_one[5], local_one[6], local_two[5], local_two[6], key_last),
        "seq",
        join_states,
        identity,
    )
    use_state = (segment_ids.astype(jnp.float32) == incoming[4][:, None]).astype(jnp.float32)

    def far_finish(local_part, state_in, norm_in):
        feat_q = local_part[0].astype(jnp.float32)
        numer = local_part[3] + use_state[:, :, None, None] * jnp.einsum(
            "rqhe,rhef->rqhf", feat_q, state_in, precision=EXACT_PRECISION
        )
        denom = local_part[4] + use_state[:, :, None] * jnp.einsum(
            "rqhe,rhe->rqh", feat_q, norm_in, precision=EXACT_PRECISION
        )
        return (numer / denom[..., None], denom)

    far_one, denom_one = far_finish(local_one, incoming[0], incoming[1])
    far_two, denom_two = far_finish(local_two, incoming[2], incoming[3])
    blended = (
        near_out + blend[0][None, None, :, None] * far_one + blend[1][None, None, :, None] * far_two
    )
    mixed_low = blended.astype(jnp.bfloat16).reshape(total_rows, D)
    branch = jnp.dot(mixed_low, w_out, preferred_element_type=jnp.float32)
    middle = inputs + branch
    normed_two, inverse_two = norm_apply(middle, gain_two)
    normed_two_low = normed_two.astype(jnp.bfloat16)
    upward_value = jnp.dot(normed_two_low, w_up, preferred_element_type=jnp.float32)
    active, gelu_pull = jax.vjp(gelu_value, upward_value)
    active_low = active.astype(jnp.bfloat16)
    output = middle + jnp.dot(active_low, w_down, preferred_element_type=jnp.float32)
    output_low = output.astype(jnp.bfloat16).reshape(row_count, tok_count, D)
    grad_in = cotangent.reshape(total_rows, D)
    grad_down = jnp.dot(active_low.T, grad_in, preferred_element_type=jnp.float32)
    grad_active = jnp.dot(grad_in, w_down.T, preferred_element_type=jnp.float32)
    grad_upval = gelu_pull(grad_active)[0].astype(jnp.bfloat16)
    grad_up = jnp.dot(normed_two_low.T, grad_upval, preferred_element_type=jnp.float32)
    grad_normed_two = jnp.dot(grad_upval, w_up.T, preferred_element_type=jnp.float32)
    grad_gain_two = jnp.sum(grad_normed_two * middle * inverse_two, 0)
    grad_middle = grad_in.astype(jnp.float32) + norm_back(
        middle, inverse_two, gain_two, grad_normed_two
    )
    mlp_sums = (grad_down, grad_up, grad_gain_two)
    grad_branch = grad_middle.astype(jnp.bfloat16)
    grad_out = jnp.dot(mixed_low.T, grad_branch, preferred_element_type=jnp.float32)
    grad_mixed = (
        jnp.dot(grad_branch, w_out.T, preferred_element_type=jnp.float32)
        .astype(jnp.bfloat16)
        .reshape(row_count, tok_count, H, E)
    )
    grad_mixed_full = grad_mixed.astype(jnp.float32)
    grad_blend = jnp.stack(
        [
            jnp.einsum("rqhe,rqhe->h", grad_mixed_full, far_one),
            jnp.einsum("rqhe,rqhe->h", grad_mixed_full, far_two),
        ],
        0,
    )
    scores = near_scores()
    weights = jnp.exp(scores - log_total)
    grad_weights = jnp.einsum(
        "rqhe,rkhe->rhqk", grad_mixed, wide_values, preferred_element_type=jnp.float32
    )
    row_delta = jnp.sum(weights * grad_weights, -1, keepdims=True)
    grad_scores = (weights * (grad_weights - row_delta)).astype(jnp.bfloat16)
    near_dq = (
        jnp.einsum("rhqk,rkhe->rqhe", grad_scores, wide_keys, preferred_element_type=jnp.float32)
        * score_scale
    )
    wide_dk = (
        jnp.einsum("rhqk,rqhe->rkhe", grad_scores, queries, preferred_element_type=jnp.float32)
        * score_scale
    )
    wide_dv = jnp.einsum(
        "rhqk,rqhe->rkhe",
        weights.astype(jnp.bfloat16),
        grad_mixed,
        preferred_element_type=jnp.float32,
    )
    back_keys, back_values = (
        shifted(wide_dk[:, :BAND].astype(jnp.bfloat16), "seq", -1).astype(jnp.float32),
        shifted(wide_dv[:, :BAND].astype(jnp.bfloat16), "seq", -1).astype(jnp.float32),
    )
    near_dk = jnp.concatenate([wide_dk[:, BAND:tok_count], wide_dk[:, tok_count:] + back_keys], 1)
    near_dv = jnp.concatenate([wide_dv[:, BAND:tok_count], wide_dv[:, tok_count:] + back_values], 1)

    def far_back(local_part, far_val, denom, blend_row, state_in, norm_in):
        feat_q = local_part[0].astype(jnp.float32)
        kernel = local_part[2]
        grad_far = blend_row[None, None, :, None] * grad_mixed_full
        grad_numer = grad_far / denom[..., None]
        numer_low = grad_numer.astype(jnp.bfloat16)
        grad_denom = -jnp.sum(grad_far * far_val, -1) / denom
        grad_kernel = (
            jnp.einsum("rqhe,rkhe->rhqk", numer_low, value_rows, preferred_element_type=jnp.float32)
            + jnp.transpose(grad_denom, (0, 2, 1))[..., None]
        ).astype(jnp.bfloat16) * far_mask_low
        value_part = jnp.einsum(
            "rhqk,rqhe->rkhe", kernel, numer_low, preferred_element_type=jnp.float32
        )
        grad_feat_q = jnp.einsum(
            "rhqk,rkhe->rqhe", grad_kernel, local_part[1], preferred_element_type=jnp.float32
        ) + use_state[:, :, None, None] * (
            jnp.einsum("rqhf,rhef->rqhe", grad_numer, state_in, precision=EXACT_PRECISION)
            + grad_denom[..., None] * norm_in[:, None]
        )
        grad_feat_k = jnp.einsum(
            "rhqk,rqhe->rkhe", grad_kernel, local_part[0], preferred_element_type=jnp.float32
        )
        used_q = feat_q * use_state[:, :, None, None]
        grad_state = jnp.einsum("rqhe,rqhf->rhef", used_q, grad_numer, precision=EXACT_PRECISION)
        grad_norm = jnp.einsum("rqhe,rqh->rhe", used_q, grad_denom, precision=EXACT_PRECISION)
        return (grad_feat_q, grad_feat_k, value_part, grad_state, grad_norm)

    back_one = far_back(local_one, far_one, denom_one, blend[0], incoming[0], incoming[1])
    back_two = far_back(local_two, far_two, denom_two, blend[1], incoming[2], incoming[3])
    key_first = segment_ids[:, 0].astype(jnp.float32)
    returned = prefix_2(
        (back_one[3], back_one[4], back_two[3], back_two[4], key_first),
        "seq",
        join_states,
        identity,
    )
    hit_state = (returned[4] == key_last).astype(jnp.float32)

    def far_close(local_part, back_part, state_grad_in, norm_grad_in, slope):
        feat_k = local_part[1].astype(jnp.float32)
        state_grad = hit_state[:, None, None, None] * state_grad_in
        norm_grad = hit_state[:, None, None] * norm_grad_in
        tail_col = tail_weight[:, :, None, None]
        grad_feat_k = back_part[1] + tail_col * (
            jnp.einsum("rhef,rkhf->rkhe", state_grad, value_full, precision=EXACT_PRECISION)
            + norm_grad[:, None]
        )
        value_part = back_part[2] + tail_col * jnp.einsum(
            "rhef,rkhe->rkhf", state_grad, feat_k, precision=EXACT_PRECISION
        )
        return (back_part[0] * slope(query_full), grad_feat_k * slope(key_full), value_part)

    far_dq_one, far_dk_one, far_dv_one = far_close(
        local_one, back_one, returned[0], returned[1], slope_one
    )
    far_dq_two, far_dk_two, far_dv_two = far_close(
        local_two, back_two, returned[2], returned[3], slope_two
    )
    grad_queries = (near_dq + far_dq_one + far_dq_two).astype(jnp.bfloat16).reshape(total_rows, D)
    grad_keys = (near_dk + far_dk_one + far_dk_two).astype(jnp.bfloat16).reshape(total_rows, D)
    grad_values = (near_dv + far_dv_one + far_dv_two).astype(jnp.bfloat16).reshape(total_rows, D)
    grad_query = jnp.dot(normed_low.T, grad_queries, preferred_element_type=jnp.float32)
    grad_key = jnp.dot(normed_low.T, grad_keys, preferred_element_type=jnp.float32)
    grad_value = jnp.dot(normed_low.T, grad_values, preferred_element_type=jnp.float32)
    grad_normed = jnp.dot(grad_queries, w_query.T, preferred_element_type=jnp.float32)
    grad_normed = grad_normed + jnp.dot(grad_keys, w_key.T, preferred_element_type=jnp.float32)
    grad_normed = grad_normed + jnp.dot(grad_values, w_value.T, preferred_element_type=jnp.float32)
    grad_gain_one = jnp.sum(grad_normed * inputs * inverse_one, 0)
    grad_inputs = grad_middle + norm_back(inputs, inverse_one, gain_one, grad_normed)
    grad_tokens = grad_inputs.astype(jnp.bfloat16).reshape(row_count, tok_count, D)
    summed = lax.psum(
        (
            grad_query,
            grad_key,
            grad_value,
            grad_out,
            grad_gain_one,
            grad_blend,
            mlp_sums[0],
            mlp_sums[1],
            mlp_sums[2],
        ),
        ("seq", "rows"),
    )
    return (
        output_low,
        grad_tokens,
        summed[4],
        summed[0],
        summed[1],
        summed[2],
        summed[5],
        summed[3],
        summed[8],
        summed[7],
        summed[6],
    )


def solution(mesh):
    return jax.shard_map(
        shards,
        mesh=mesh,
        in_specs=(
            P("rows", "seq", None),
            P("rows", "seq"),
            P("rows", "seq"),
            P(),
            P(),
            P(),
            P(),
            P(),
            P(),
            P(),
            P(),
            P(),
            P("rows", "seq", None),
        ),
        out_specs=(
            P("rows", "seq", None),
            P("rows", "seq", None),
            P(),
            P(),
            P(),
            P(),
            P(),
            P(),
            P(),
            P(),
            P(),
        ),
        check_vma=False,
    )
```

profile of v0, /device:TPU:1, one launch (start us, length us, event | category | flops | bytes accessed | tf_op | source)
XLA Modules:
  0.0 613.0 jit_solution(18327345524190609837)
XLA Ops:
  23.2 4.5 collective-permute-start.1
  28.6 3.5 collective-permute-start
  33.0 3.1 collective-permute-start.2
  41.6 27.9 %all-reduce.4 = (bf16[24]{0:T(256)(128)(2,1)S(1)}, bf16[24]{0:T(256)(128)(2,1)S(1)}) all-reduce(bf16[24]{0:T(256)(128)(2,1)S(1)} %dynamic-update-slice, bf16[24]{0:T(256)(128)(2,1)S(1)} %dynamic-update-slice.1), channel_id=2, replica_groups=mesh['seq'=8,'rows'=4] {'seq'}, use_global_device_ids=true, to_apply=%add | all-reduce | flops 48 | bytes 192
  77.6 24.3 %all-gather.4 = bf16[24,8,64]{2,1,0:T(8,128)(2,1)S(1)} all-gather(bf16[3,8,64]{2,1,0:T(8,128)(2,1)S(1)} %get-tuple-element.427), channel_id=6, replica_groups=mesh['seq'=8,'rows'=4] {'seq'}, dimensions={0}, use_global_device_ids=true | all-gather | bytes 27648 | tf_op jit(solution)/shard_map/all_gather | solution.py:28
  102.0 24.4 %all-gather.2 = bf16[24,8,64]{2,1,0:T(8,128)(2,1)S(1)} all-gather(bf16[3,8,64]{2,1,0:T(8,128)(2,1)S(1)} %get-tuple-element.428), channel_id=4, replica_groups=mesh['seq'=8,'rows'=4] {'seq'}, dimensions={0}, use_global_device_ids=true | all-gather | bytes 27648 | tf_op jit(solution)/shard_map/all_gather | solution.py:28
  127.3 2.6 convert_reduce_fusion.1
  134.4 2.7 fusion.198
  143.9 13.5 %all-gather.15.cloned.1.call-done = bf16[24,8,64,64]{3,2,1,0:T(8,128)(2,1)} async-done(((bf16[3,8,64,64]{3,2,1,0:T(8,128)(2,1)}), bf16[24,8,64,64]{3,2,1,0:T(8,128)(2,1)}) %all-gather.15.cloned.1.call-update) | async-done | bytes 1572880 | tf_op jit(solution)/shard_map/all_gather | solution.py:28
  157.4 24.8 %while.43 = (s32[]{:T(128)}, f32[3,8,64,64]{3,2,1,0:T(8,128)}, f32[3,8,64]{2,1,0:T(8,128)S(1)}, f32[3,8,64,64]{3,2,1,0:T(8,128)S(1)}, f32[3,8,64]{2,1,0:T(8,128)...) while((s32[]{:T(128)}, f32[3,8,64,64]{3,2,1,0:T(8,128)}, ...), condition=%wide.region_6.7_spmd.clone, body=%wide.region_5.6_spmd.clone.sunk | while | flops 1198114 | bytes 1997075 | solution.py:45
  158.0 2.7 select_select_fusion.6
  160.8 3.0 select_select_fusion.6
  163.9 3.0 select_select_fusion.6
  167.0 3.0 select_select_fusion.6
  170.1 3.0 select_select_fusion.6
  173.1 3.0 select_select_fusion.6
  176.2 3.0 select_select_fusion.6
  179.3 3.0 select_select_fusion.6
  191.4 4.1 fusion.15
  198.4 2.4 convolution_convert_fusion.1
  203.8 2.3 convolution_convert_fusion
  211.5 3.2 fusion.27
  231.1 3.4 fusion.170
  234.5 3.5 fusion.185
  243.2 38.1 %all-gather.7 = bf16[24,8,64]{2,1,0:T(8,128)(2,1)S(1)} all-gather(bf16[3,8,64]{2,1,0:T(8,128)(2,1)S(1)} %convert_element_type.431), channel_id=9, replica_groups=mesh['seq'=8,'rows'=4] {'seq'}, dimensions={0}, use_global_device_ids=true | all-gather | bytes 27648 | tf_op jit(solution)/shard_map/all_gather | solution.py:53
  281.3 24.7 %all-gather.9 = bf16[24,8,64]{2,1,0:T(8,128)(2,1)S(1)} all-gather(bf16[3,8,64]{2,1,0:T(8,128)(2,1)S(1)} %convert_element_type.434), channel_id=11, replica_groups=mesh['seq'=8,'rows'=4] {'seq'}, dimensions={0}, use_global_device_ids=true | all-gather | bytes 27648 | tf_op jit(solution)/shard_map/all_gather | solution.py:53
  308.1 26.7 %all-gather.21.cloned.1.call-done = bf16[24,8,64,64]{3,2,1,0:T(8,128)(2,1)} async-done(((bf16[3,8,64,64]{3,2,1,0:T(8,128)(2,1)}), bf16[24,8,64,64]{3,2,1,0:T(8,128)(2,1)}) %all-gather.21.cloned.1.call-update) | async-done | bytes 1572880 | tf_op jit(solution)/shard_map/all_gather | solution.py:53
  335.0 13.3 %while.42 = (s32[]{:T(128)}, f32[3,8,64,64]{3,2,1,0:T(8,128)S(1)}, f32[3,8,64]{2,1,0:T(8,128)S(1)}, f32[3,8,64,64]{3,2,1,0:T(8,128)S(1)}, f32[3,8,64]{2,1,0:T(8,...) while((s32[]{:T(128)}, f32[3,8,64,64]{3,2,1,0:T(8,128)S(1)}, ...), condition=%wide.region_15.16_spmd, body=%wide.region_14.15_spmd.sunk | while | flops 798747 | bytes 1997112 | solution.py:70
  362.9 4.5 fusion.50
  369.3 39.6 %all-reduce.2 = (f32[512]{0:T(512)}, f32[2,8]{1,0:T(2,128)}, f32[512]{0:T(512)}) all-reduce(f32[512]{0:T(512)S(1)} %get-tuple-element.421, f32[2,8]{1,0:T(2,128)S(1)} %pad_maximum_fusion.7, f32[512]{0:T(512)S(1)} %get-tuple-element.419), channel_id=1, replica_groups=mesh['seq'=8,'rows'=4] {'seq','rows'}, use_global_device_ids=true, to_apply=%region_18.19 | all-reduce | flops 1040 | bytes 8320 | tf_op jit(solution)/shard_map/psum | solution.py:404
  409.9 183.8 %all-reduce.7.cloned.1.call-done = (f32[512,512]{1,0:T(8,128)}, f32[512,512]{1,0:T(8,128)}, f32[512,512]{1,0:T(8,128)}, f32[512,512]{1,0:T(8,128)}, f32[512,2048]{1,0:T(8,128)}, /*index=5*/f32[2048,512]{1,0:T(8,128)}) async-done(((f32[512,512]{1,0:T(8,128)}, f32[512,512]{1,0:T(8,128)}, f32[512,512]{1,0:T(8,128)}, f32[512,512]{1,0:T(8,128)}, f32[512,2048]{1,0:T(8,128)}, /*index=5*/f32[2048,512]{1,0:T(8,128)}), ...) | async-done | bytes 12582928 | tf_op jit(solution)/shard_map/psum | solution.py:404
  593.7 2.4 copy.267
  (380 shorter events, 127.3 us)
Async XLA Ops:
  7.2 184.3 %copy-start = (bf16[512,2048]{1,0:T(8,128)(2,1)S(1)}, bf16[512,2048]{1,0:T(8,128)(2,1)}, u32[]{:S(2)}) copy-start(bf16[512,2048]{1,0:T(8,128)(2,1)} %param.27) | copy-start | bytes 6291460
  7.2 136.7 %all-gather.17.cloned.1.call-start = ((), (), s32[]{:S(2)}) async-start(), calls=%async_computation.1 | async-start | bytes 3538944 | tf_op jit(solution)/shard_map/all_gather | solution.py:28
  8.2 13.0 %copy-start.85 = (s32[3]{0:T(128)}, s32[3]{0:T(128)S(1)}, u32[]{:S(2)}) copy-start(s32[3]{0:T(128)S(1)} %slice_reduce_fusion) | copy-start | bytes 40
  9.0 28.6 %copy-start.82 = (pred[3,128]{1,0:T(4,128)(4,1)}, pred[3,128]{1,0:T(4,128)(4,1)S(1)}, u32[]{:S(2)}) copy-start(pred[3,128]{1,0:T(4,128)(4,1)S(1)} %get-tuple-element.491) | copy-start | bytes 1156
  10.7 5.6 copy-start.47
  11.9 5.5 copy-start.30
  16.3 22.5 %copy-start.7 = (bf16[3,128,8,64]{1,3,2,0:T(8,128)(2,1)}, bf16[3,128,8,64]{1,3,2,0:T(8,128)(2,1)S(1)}, u32[]{:S(2)}) copy-start(bf16[3,128,8,64]{1,3,2,0:T(8,128)(2,1)S(1)} %copy.90) | copy-start | bytes 1179652
  16.3 4.9 copy-start.71
  22.5 134.9 %all-gather.15.cloned.1.call-start = ((), (), s32[]{:S(2)}) async-start(), calls=%async_computation | async-start | bytes 3538944 | tf_op jit(solution)/shard_map/all_gather | solution.py:28
  23.2 114.6 %collective-permute-start.1 = (bf16[3,30]{1,0:T(4,128)(2,1)}, bf16[3,30]{1,0:T(4,128)(2,1)}, u32[]{:S(2)}, u32[]{:S(2)}) collective-permute-start(bf16[3,30]{1,0:T(4,128)(2,1)} %slice.45), channel_id=1, source_target_pairs={{0,4},{4,8},{8,12},{12,16},{16,20},{20,24},{24,28},{1,5},{5,9},{9,... | collective-permute-start | bytes 548 | tf_op jit(solution)/shard_map/ppermute | solution.py:22
  28.6 10.7 %copy-start.87 = (f32[2,8]{1,0:T(2,128)S(1)}, f32[2,8]{1,0:T(2,128)}, u32[]{:S(2)}) copy-start(f32[2,8]{1,0:T(2,128)} %param.24) | copy-start | bytes 196
  28.6 11.2 %copy-start.88 = (u32[32]{0:T(128)S(1)}, u32[32]{0:T(128)}, u32[]{:S(2)}) copy-start(u32[32]{0:T(128)} %constant.130) | copy-start | bytes 388
  28.6 159.0 %collective-permute-start = (bf16[3,30,8,64]{1,3,2,0:T(8,128)(2,1)}, bf16[3,30,8,64]{1,3,2,0:T(8,128)(2,1)}, u32[]{:S(2)}, u32[]{:S(2)}) collective-permute-start(bf16[3,30,8,64]{1,3,2,0:T(8,128)(2,1)} %slice.57), channel_id=1, source_target_pairs={{0,4},{4,8},{8,12},{12,16},{16,20},{20,24},{24,28},{1,5},{5,9},{9,... | collective-permute-start | bytes 276488 | tf_op jit(solution)/shard_map/ppermute | solution.py:22
  33.0 107.0 %collective-permute-start.2 = (bf16[3,30,8,64]{1,3,2,0:T(8,128)(2,1)}, bf16[3,30,8,64]{1,3,2,0:T(8,128)(2,1)}, u32[]{:S(2)}, u32[]{:S(2)}) collective-permute-start(bf16[3,30,8,64]{1,3,2,0:T(8,128)(2,1)} %slice.58), channel_id=1, source_target_pairs={{0,4},{4,8},{8,12},{12,16},{16,20},{20,24},{24,28},{1,5},{5,9},{9,... | collective-permute-start | bytes 276488 | tf_op jit(solution)/shard_map/ppermute | solution.py:22
  37.3 270.8 %all-gather.19.cloned.1.call-start = ((), (), s32[]{:S(2)}) async-start(), calls=%async_computation.2 | async-start | bytes 3538944 | tf_op jit(solution)/shard_map/all_gather | solution.py:53
  140.0 17.4 %copy-start.78 = (bf16[8,3]{1,0:T(8,128)(2,1)S(1)}, bf16[8,3]{1,0:T(8,128)(2,1)}, u32[]{:S(2)}) copy-start(bf16[8,3]{1,0:T(8,128)(2,1)} %reshape.397) | copy-start | bytes 148
  186.3 4.9 copy-start.20
  191.1 5.7 copy-start.42
  198.4 11.1 %copy-start.13 = (bf16[3,128,8,64]{1,0,3,2:T(4,128)(2,1)}, bf16[3,128,8,64]{1,0,3,2:T(4,128)(2,1)S(1)}, u32[]{:S(2)}) copy-start(bf16[3,128,8,64]{1,0,3,2:T(4,128)(2,1)S(1)} %reshape.382) | copy-start | bytes 1179652
  200.8 134.0 %all-gather.21.cloned.1.call-start = ((), (), s32[]{:S(2)}) async-start(), calls=%async_computation.3 | async-start | bytes 3538944 | tf_op jit(solution)/shard_map/all_gather | solution.py:53
  216.6 377.1 %all-reduce.7.cloned.1.call-start = ((), (), s32[]{:S(2)}) async-start(), calls=%async_computation.4 | async-start | bytes 25165824 | tf_op jit(solution)/shard_map/psum | solution.py:404
  223.7 3.7 copy-start.24
  223.7 5.2 copy-start.11
  223.7 5.2 copy-start.52
  224.4 4.5 copy-start.33
  224.5 81.5 %collective-permute-start.4 = (bf16[3,30,8,64]{1,3,2,0:T(8,128)(2,1)S(1)}, bf16[3,30,8,64]{1,3,2,0:T(8,128)(2,1)S(1)}, u32[]{:S(2)}, u32[]{:S(2)}) collective-permute-start(bf16[3,30,8,64]{1,3,2,0:T(8,128)(2,1)S(1)} %slice.78), channel_id=1, source_target_pairs={{4,0},{8,4},{12,8},{16,12},{20,16},{24,20},{28,24},{5,1},{9,5},{13... | collective-permute-start | bytes 276488 | tf_op jit(solution)/shard_map/ppermute | solution.py:22
  242.0 65.1 %collective-permute-start.3 = (bf16[3,30,8,64]{1,3,2,0:T(8,128)(2,1)S(1)}, bf16[3,30,8,64]{1,3,2,0:T(8,128)(2,1)S(1)}, u32[]{:S(2)}, u32[]{:S(2)}) collective-permute-start(bf16[3,30,8,64]{1,3,2,0:T(8,128)(2,1)S(1)} %slice.79), channel_id=1, source_target_pairs={{4,0},{8,4},{12,8},{16,12},{20,16},{24,20},{28,24},{5,1},{9,5},{13... | collective-permute-start | bytes 276488 | tf_op jit(solution)/shard_map/ppermute | solution.py:22
  307.1 27.9 %copy-start.77 = (bf16[8,3]{1,0:T(8,128)(2,1)S(1)}, bf16[8,3]{1,0:T(8,128)(2,1)}, u32[]{:S(2)}) copy-start(bf16[8,3]{1,0:T(8,128)(2,1)} %reshape.402) | copy-start | bytes 148
  335.0 13.4 %copy-start.86 = (s32[3]{0:T(128)S(1)}, s32[3]{0:T(128)}, u32[]{:S(2)}) copy-start(s32[3]{0:T(128)} %copy-done.85) | copy-start | bytes 40
  362.9 4.5 copy-start.45
  367.4 41.5 %copy-start.12 = (f32[384,512]{1,0:T(8,128)S(1)}, f32[384,512]{1,0:T(8,128)}, u32[]{:S(2)}) copy-start(f32[384,512]{1,0:T(8,128)} %copy-done.10) | copy-start | bytes 2359300
  593.7 4.4 copy-start.58
  (69 other events, 141.0 us)
Sparse Core Ops, SparseCore 0:
  22.6 72.5 all-gather.16
  98.0 59.4 all-gather.14
  201.0 71.6 all-gather.18
  274.7 60.0 all-gather.20
  359.1 234.5 all-reduce.6
where the time goes:
time: 624 us; the launch traced here: 613 us
  waiting for transfers between devices  224 us (36%)
  blocking collectives  179 us (29%)
  matrix products  80.4 us (13%)
  other arithmetic  53.2 us (9%)
  local copies, waits for them, and re-layouts  44.9 us (7%)
  between operations  16 us (3%)
  starting transfers between devices  14.3 us (2%)
    psum x1, waiting for transfers between devices, shards(): lax.psum((grad_query, grad_key, grad_value, grad_out, grad_gain_one, grad...  184 us
    all_gather x2, blocking collectives, prefix_2(): lax.all_gather(a.astype(kind), axis)  62.8 us
    all_gather x2, blocking collectives, prefix(): lax.all_gather(part.astype(kind), axis)  48.8 us
    psum x1, blocking collectives, shards(): lax.psum((grad_query, grad_key, grad_value, grad_out, grad_gain_one, grad...  39.6 us
    unnamed x1, blocking collectives  27.9 us
    all_gather x2, waiting for transfers between devices, prefix_2(): lax.all_gather(a.astype(kind), axis)  26.7 us
    select_n x24, other arithmetic, turn(): return jax.tree.map(lambda a, b: jnp.where(reached, a, b), new, before)  24.2 us
    unnamed x193, local copies, waits for them, and re-layouts  23.5 us
  transfers between devices with their start and end apart: 10, of which 3 were waited for; matrix products, arithmetic and copies ran while one was open for 18% of the time, Pallas kernels for 0%

commit v1 on v0

v1 whole, which is shorter than its diff:
```python
import functools
import math

import jax
import jax.numpy as jnp
from jax import lax
from jax.experimental import pallas as pl
from jax.experimental.pallas import tpu as pltpu
from jax.sharding import PartitionSpec as P

MESH = pl.DeviceIdType.MESH
F32 = jnp.float32
BF = jnp.bfloat16
D = 512
H = 8
E = 64
FF = 2048
BAND = 30
T = 128
PAIRS = 4
PAY = 144
HALO = 32
EPSILON = 1e-06
NEGATIVE = -1e30
SCALE = 1.0 / math.sqrt(E)
GELU_A = math.sqrt(2.0 / math.pi)
GELU_B = 0.044715
ROW_UP = FF
ROW_OUT = 2 * FF
ROW_Q = ROW_OUT + D
ROW_SMALL = ROW_Q + 3 * D
SMALL = 16
ROWS_ALL = ROW_SMALL + SMALL


def nn(a, b):
    return lax.dot_general(a, b, (((1,), (0,)), ((), ())), preferred_element_type=F32)


def nt(a, b):
    return lax.dot_general(a, b, (((1,), (1,)), ((), ())), preferred_element_type=F32)


def tn(a, b):
    return lax.dot_general(a, b, (((0,), (0,)), ((), ())), preferred_element_type=F32)


def lane_low(rows):
    return lax.broadcasted_iota(jnp.int32, (rows, T), 1) < E


def low_high():
    low = lane_low(T).astype(F32)
    return low.astype(BF), (1.0 - low).astype(BF)


def two_blocks(x):
    low, high = low_high()
    rows = x.shape[0]
    return jnp.concatenate([x * low[:rows], x * high[:rows]], 0)


def pick(stacked):
    half = stacked.shape[0] // 2
    return jnp.where(lane_low(half), stacked[:half], stacked[half:])


def block_ones():
    i = lax.broadcasted_iota(jnp.int32, (T, T), 0) < E
    j = lax.broadcasted_iota(jnp.int32, (T, T), 1) < E
    return jnp.where(i == j, 1.0, 0.0).astype(BF)


def feature_one(t):
    return jnp.where(t > 0, t + 1.0, jnp.exp(jnp.minimum(t, 0.0)))


def slope_one(t):
    return jnp.where(t > 0, 1.0, jnp.exp(jnp.minimum(t, 0.0)))


def feature_two(t):
    return 1.0 + jnp.tanh(t)


def slope_two(t):
    tangent = jnp.tanh(t)
    return 1.0 - tangent * tangent


FEATURES = ((feature_one, slope_one), (feature_two, slope_two))


def layer_kernel(
    n,
    R,
    tok,
    seg,
    pad,
    gain_one,
    gain_two,
    blend,
    w_query,
    w_key,
    w_value,
    w_out_hbm,
    w_up_hbm,
    w_down_hbm,
    cot_hbm,
    out,
    grad_tok,
    grads,
    w_out,
    w_up,
    w_down,
    cot,
    normed,
    normed_two,
    mixed,
    middle,
    total,
    back_two,
    q_s,
    k_s,
    v_s,
    hk_s,
    hv_s,
    fq_s,
    fk_s,
    kk_s,
    p_s,
    ph_s,
    near_s,
    far_s,
    den_s,
    db_s,
    low_s,
    dden_s,
    dq_s,
    dk_s,
    dv_s,
    hdk_s,
    hdv_s,
    hdk_r,
    hdv_r,
    wide_s,
    far_mask,
    near_mask,
    use_mask,
    tail_mask,
    halo_mask,
    info_own,
    info_in,
    gb_s,
    pay_s,
    m1_r,
    sum_s,
    carry_r,
    pass_s,
    in_s,
    give_s,
    w_sem,
    info_send,
    info_recv,
    halo_send,
    halo_recv,
    chain_send,
    chain_recv,
):
    U = R * PAIRS
    HU = U // 2
    sq = lax.axis_index("seq")
    rw = lax.axis_index("rows")
    par = lax.rem(sq, 2)
    z = sq // 2
    nz = n // 2
    partner = sq + 1 - 2 * par

    def unit_row(u):
        return lax.rem(u, 2 * R) // 2

    def unit_pair(u):
        return (u // (2 * R)) * 2 + lax.rem(u, 2)

    def unit_of(r, hp):
        return (hp // 2) * 2 * R + r * 2 + hp % 2

    def send(src, dst, send_sem, recv_sem, to):
        return pltpu.make_async_remote_copy(
            src_ref=src,
            dst_ref=dst,
            send_sem=send_sem,
            recv_sem=recv_sem,
            device_id=(to, rw),
            device_id_type=MESH,
        )

    barrier = pltpu.get_barrier_semaphore()
    for step in (1, 2):

        @pl.when(sq >= step)
        def _():
            pl.semaphore_signal(barrier, inc=1, device_id=(sq - step, rw), device_id_type=MESH)

        @pl.when(sq + step < n)
        def _():
            pl.semaphore_signal(barrier, inc=1, device_id=(sq + step, rw), device_id_type=MESH)

    loads = [
        pltpu.make_async_copy(src, dst, w_sem.at[i])
        for i, (src, dst) in enumerate(
            ((w_out_hbm, w_out), (w_up_hbm, w_up), (w_down_hbm, w_down), (cot_hbm, cot))
        )
    ]
    for load in loads:
        load.start()

    for r in range(R):
        rows = pl.ds(r * T, T)
        x = tok[rows, :].astype(F32)
        inverse = lax.rsqrt(jnp.mean(x * x, -1, keepdims=True) + EPSILON)
        normed[rows, :] = (x * inverse * gain_one[...]).astype(BF)
    for weight, held in ((w_key, k_s), (w_value, v_s), (w_query, q_s)):
        whole = nn(normed[...], weight[...]).astype(BF)
        for r in range(R):
            for hp in range(PAIRS):
                held[unit_of(r, hp)] = whole[r * T : (r + 1) * T, hp * T : (hp + 1) * T]

    i_pos = lax.broadcasted_iota(jnp.int32, (T, T), 0)
    j_pos = lax.broadcasted_iota(jnp.int32, (T, T), 1)
    info_own[...] = jnp.zeros_like(info_own)
    for r in range(R):
        seg_row = seg[r : r + 1, :].astype(F32)
        pad_row = pad[r : r + 1, :].astype(F32)
        seg_j = jnp.broadcast_to(seg_row, (T, T))
        pad_j = jnp.broadcast_to(pad_row, (T, T))
        seg_i = seg_j.T
        pad_i = pad_j.T
        same = seg_i == seg_j
        open_key = same & (((j_pos < i_pos) & (pad_j == 1.0)) | (i_pos == j_pos))
        far_mask[r] = open_key.astype(F32)
        near_mask[r] = (open_key & (i_pos - j_pos <= BAND)).astype(F32)
        last = seg_i[T - 1 : T, :]
        tail_mask[r] = ((seg_i == last) & (pad_i == 1.0)).astype(F32)
        use_mask[r] = seg_i
        info_own[0, r : r + 1, :] = last
        info_own[1, r : r + 1, :] = jnp.where(pad_row == 1.0, seg_row + 1.0, 0.0)

    head = pl.ds(0, T - HALO)
    hk_s[:, head, :] = jnp.zeros((U, T - HALO, T), BF)
    hv_s[:, head, :] = jnp.zeros((U, T - HALO, T), BF)

    @pl.when(sq == 0)
    def _():
        tail = pl.ds(T - HALO, HALO)
        hk_s[:, tail, :] = jnp.zeros((U, HALO, T), BF)
        hv_s[:, tail, :] = jnp.zeros((U, HALO, T), BF)

    @pl.when(sq == n - 1)
    def _():
        hdk_r[...] = jnp.zeros((U, HALO, T), BF)
        hdv_r[...] = jnp.zeros((U, HALO, T), BF)

    pl.semaphore_wait(barrier, jnp.minimum(sq, 2) + jnp.minimum(n - 1 - sq, 2))

    def info_copy(slot, to):
        return send(info_own, info_in.at[slot], info_send.at[slot], info_recv.at[slot], to)

    def halo_copy(which, to):
        src, dst = ((k_s, hk_s), (v_s, hv_s))[which]
        tail = pl.ds(T - HALO, HALO)
        return send(
            src.at[:, tail, :], dst.at[:, tail, :], halo_send.at[which], halo_recv.at[which], to
        )

    for slot, step in enumerate((1, 2, -1)):
        inside = (sq + step >= 0) & (sq + step < n)
        came = (sq - step >= 0) & (sq - step < n)

        @pl.when(inside)
        def _():
            info_copy(slot, sq + step).start()

        @pl.when(jnp.logical_not(came))
        def _():
            info_in[slot, 0] = jnp.full((8, T), -1.0, F32)
            info_in[slot, 1] = jnp.zeros((8, T), F32)

    @pl.when(sq + 1 < n)
    def _():
        for which in range(2):
            halo_copy(which, sq + 1).start()

    ones_block = block_ones()

    def local_state(u, _):
        r = unit_row(u)
        tail = tail_mask[r].astype(BF)
        keys = k_s[u].astype(F32)
        values = v_s[u]
        norms = []
        for a, (feature, _slope) in enumerate(FEATURES):
            fk = feature(keys).astype(BF)
            fk_s[a, u] = fk
            weighted = fk * tail
            pay_s[0, u, a * E : (a + 1) * E, :] = pick(tn(weighted, values)).astype(BF)
            norm = jnp.sum(weighted.astype(F32), 0, keepdims=True)
            norms.append(jnp.broadcast_to(norm, (8, T)))
        pay_s[0, u, 2 * E : PAY, :] = jnp.concatenate(norms, 0).astype(BF)
        return 0

    lax.fori_loop(0, U, local_state, 0)

    def half(which, r):
        return pl.ds(which * HU + 2 * r, 2)

    def chain_copy(way, stage, r):
        step = 1 - 2 * way
        here = pl.ds(2 * r, 2)
        src, dst, to = (
            (pay_s.at[way, half(1 - par, r)], m1_r.at[way, here], partner),
            (pass_s.at[way, here], carry_r.at[way, here], sq + 2 * step),
            (give_s.at[way, here], in_s.at[way, half(par, r)], partner),
        )[stage]
        return send(src, dst, chain_send.at[way, stage, r], chain_recv.at[way, stage, r], to)

    def chain_arrival(way, stage, r):
        here = pl.ds(2 * r, 2)
        dst = (m1_r.at[way, here], carry_r.at[way, here], in_s.at[way, half(1 - par, r)])[stage]
        return send(dst, dst, chain_send.at[way, stage, r], chain_recv.at[way, stage, r], partner)

    def has_next(way):
        return (z + 1 < nz) if way == 0 else (z > 0)

    def has_before(way):
        return (z > 0) if way == 0 else (z + 1 < nz)

    def marks(r):
        own = info_own[0, r : r + 1, :]
        before, before_two, after = (info_in[s, 0, r : r + 1, :] for s in range(3))
        first = par == 0
        last_a = jnp.where(first, own, before)
        last_b = jnp.where(first, after, own)
        last_z = jnp.where(first, before, before_two)
        inner = (last_a == last_b).astype(F32)
        enter = (last_z == last_a).astype(F32)
        through = (last_z == last_b).astype(F32)
        return inner, enter, through

    def chain_begin(way):
        for r in range(R):
            chain_copy(way, 0, r).start()

        @pl.when(jnp.logical_not(has_before(way)))
        def _():
            carry_r[way] = jnp.zeros((HU, PAY, T), BF)

    def chain_pair(way):
        second = par == (1 - way)
        for r in range(R):
            chain_arrival(way, 0, r).wait_recv()
            inner, enter, _through = marks(r)
            weight = inner if way == 0 else enter
            one = jnp.ones_like(weight)
            mine = jnp.where(second, one, weight)
            other = jnp.where(second, weight, one)
            for j in range(2):
                own = pay_s[way, par * HU + 2 * r + j].astype(F32)
                got = m1_r[way, 2 * r + j].astype(F32)
                sum_s[2 * r + j] = mine * own + other * got

    def chain_pass(way):
        second = par == (1 - way)
        for r in range(R):

            @pl.when(has_before(way))
            def _():
                chain_arrival(way, 1, r).wait_recv()

            inner, enter, through = marks(r)
            weight = enter if way == 0 else inner
            for j in range(2):
                carry = carry_r[way, 2 * r + j].astype(F32)
                pass_s[way, 2 * r + j] = (sum_s[2 * r + j] + through * carry).astype(BF)

            @pl.when(has_next(way))
            def _():
                chain_copy(way, 1, r).start()

            for j in range(2):
                carry = carry_r[way, 2 * r + j].astype(F32)
                own = pay_s[way, par * HU + 2 * r + j].astype(F32)
                got = m1_r[way, 2 * r + j].astype(F32)
                later = jnp.where(second, got, own) + weight * carry
                in_s[way, par * HU + 2 * r + j] = jnp.where(second, later, carry).astype(BF)
                give_s[way, 2 * r + j] = jnp.where(second, carry, later).astype(BF)
            chain_copy(way, 2, r).start()

    def chain_finish(way):
        for r in range(R):
            chain_arrival(way, 2, r).wait_recv()

    def chain_drain(way):
        for r in range(R):
            chain_copy(way, 0, r).wait_send()

            @pl.when(has_next(way))
            def _():
                chain_copy(way, 1, r).wait_send()

            chain_copy(way, 2, r).wait_send()

    chain_begin(0)

    ones_pair = two_blocks(jnp.ones((T, T), BF))

    def far_local(u, _):
        r = unit_row(u)
        queries = q_s[u].astype(F32)
        values = two_blocks(v_s[u])
        mask = far_mask[r]
        mask = jnp.concatenate([mask, mask], 1)
        for a, (feature, _slope) in enumerate(FEATURES):
            fq = feature(queries).astype(BF)
            fq_s[a, u] = fq
            kernel = (nt(fq, two_blocks(fk_s[a, u])) * mask).astype(BF)
            kk_s[a, u] = kernel
            far_s[a, u] = nn(kernel, values)
            den_s[a, u] = nn(kernel, ones_pair)
        return 0

    lax.fori_loop(0, U, far_local, 0)

    for slot, step in enumerate((1, 2, -1)):
        came = (sq - step >= 0) & (sq - step < n)

        @pl.when(came)
        def _():
            info_copy(slot, sq).wait_recv()

    @pl.when(sq > 0)
    def _():
        for which in range(2):
            halo_copy(which, sq).wait_recv()

    i_low = lax.broadcasted_iota(jnp.int32, (HALO, T), 0)
    j_low = lax.broadcasted_iota(jnp.int32, (HALO, T), 1)
    for r in range(R):
        seg_i = use_mask[r]
        marks_before = info_in[0, 1, r : r + 1, :]
        reach = j_low >= T - BAND + i_low
        halo_mask[r] = (reach & (seg_i[:HALO] + 1.0 == marks_before)).astype(F32)
        use_mask[r] = (seg_i == info_in[0, 0, r : r + 1, :]).astype(F32)

    chain_pair(0)

    def near_local(u, _):
        r = unit_row(u)
        queries = q_s[u]
        scores = nt(queries, two_blocks(k_s[u])) * SCALE
        scores_halo = nt(queries[:HALO], two_blocks(hk_s[u])) * SCALE
        open_near = near_mask[r] > 0
        open_halo = halo_mask[r] > 0
        for side in range(2):
            lanes = slice(side * T, (side + 1) * T)
            s = jnp.where(open_near, scores[:, lanes], NEGATIVE)
            sh = jnp.where(open_halo, scores_halo[:, lanes], NEGATIVE)
            peak = jnp.max(s, -1, keepdims=True)
            peak_halo = jnp.maximum(peak[:HALO], jnp.max(sh, -1, keepdims=True))
            peak = jnp.concatenate([peak_halo, peak[HALO:]], 0)
            e = jnp.exp(s - peak)
            eh = jnp.exp(sh - peak_halo)
            norm = jnp.sum(e, -1, keepdims=True)
            norm_halo = norm[:HALO] + jnp.sum(eh, -1, keepdims=True)
            inverse = 1.0 / jnp.concatenate([norm_halo, norm[HALO:]], 0)
            p_s[u, :, lanes] = e * inverse
            ph_s[u, :, lanes] = eh * inverse[:HALO]
        near_s[u] = nn(p_s[u].astype(BF), two_blocks(v_s[u]))
        near_s[u, :HALO, :] += nn(ph_s[u].astype(BF), two_blocks(hv_s[u]))
        return 0

    cut = z * U // nz
    lax.fori_loop(0, cut, near_local, 0)
    chain_pass(0)
    lax.fori_loop(cut, U, near_local, 0)
    chain_finish(0)

    def blend_lanes(a, u):
        hp = unit_pair(u)
        low = lane_low(1)
        return jnp.where(low, blend[a, 2 * hp], blend[a, 2 * hp + 1])

    def far_finish(u, _):
        r = unit_row(u)
        hp = unit_pair(u)
        use = use_mask[r]
        blended = near_s[u]
        for a in range(2):
            fq = fq_s[a, u]
            state = two_blocks(in_s[0, u, a * E : (a + 1) * E, :])
            norm = in_s[0, u, 2 * E + 8 * a : 2 * E + 8 * a + 1, :].astype(F32)
            numer = far_s[a, u] + use * nn(fq, state)
            weighted = (fq.astype(F32) * norm).astype(BF)
            denom = den_s[a, u] + use * nn(weighted, ones_block)
            far = numer / denom
            far_s[a, u] = far
            den_s[a, u] = denom
            blended = blended + blend_lanes(a, u) * far
        rows = pl.ds(pl.multiple_of(r * T, T), T)
        lanes = pl.ds(pl.multiple_of(hp * T, T), T)
        mixed[rows, lanes] = blended.astype(BF)
        return 0

    lax.fori_loop(0, U, far_finish, 0)

    loads[0].wait()
    middle[...] = tok[...].astype(F32) + nn(mixed[...], w_out[...])
    for r in range(R):
        rows = pl.ds(r * T, T)
        mid = middle[rows, :]
        inverse = lax.rsqrt(jnp.mean(mid * mid, -1, keepdims=True) + EPSILON)
        normed_two[rows, :] = (mid * inverse * gain_two[...]).astype(BF)
    total[...] = jnp.zeros_like(total)
    back_two[...] = jnp.zeros_like(back_two)
    loads[1].wait()
    loads[2].wait()
    loads[3].wait()

    def feed(t, _):
        cols = pl.ds(pl.multiple_of(t * D, D), D)
        up = nn(normed_two[...], w_up[:, cols])
        square = up * up
        tangent = jnp.tanh(GELU_A * (up + GELU_B * square * up))
        act = (0.5 * up * (1.0 + tangent)).astype(BF)
        slope = 0.5 * (1.0 + tangent) + 0.5 * up * (1.0 - tangent * tangent) * GELU_A * (
            1.0 + 3.0 * GELU_B * square
        )
        total[...] += nn(act, w_down[cols, :])
        g = cot[...]
        grads[cols, :] = tn(act, g).astype(BF)
        d_up = (nt(g, w_down[cols, :]) * slope).astype(BF)
        grads[pl.ds(pl.multiple_of(ROW_UP + t * D, D), D), :] = tn(normed_two[...], d_up).astype(BF)
        back_two[...] += nt(d_up, w_up[:, cols])
        return 0

    lax.fori_loop(0, FF // D, feed, 0)
    out[...] = (middle[...] + total[...]).astype(BF)

    gain_grad_two = jnp.zeros((1, D), F32)
    for r in range(R):
        rows = pl.ds(r * T, T)
        mid = middle[rows, :]
        inverse = lax.rsqrt(jnp.mean(mid * mid, -1, keepdims=True) + EPSILON)
        d_n = back_two[rows, :]
        gain_grad_two += jnp.sum(d_n * mid * inverse, 0, keepdims=True)
        scaled = d_n * gain_two[...]
        d_mid = (
            cot[rows, :].astype(F32)
            + inverse * scaled
            - mid * (inverse * inverse * inverse) * jnp.mean(mid * scaled, -1, keepdims=True)
        )
        total[rows, :] = d_mid
        normed_two[rows, :] = d_mid.astype(BF)
    d_branch = normed_two[...]
    grads[ROW_OUT : ROW_OUT + D, :] = tn(mixed[...], d_branch).astype(BF)
    d_blended = nt(d_branch, w_out[...]).astype(BF)
    for r in range(R):
        for hp in range(PAIRS):
            db_s[unit_of(r, hp)] = d_blended[r * T : (r + 1) * T, hp * T : (hp + 1) * T]

    gb_s[...] = jnp.zeros_like(gb_s)

    def far_prepare(u, _):
        r = unit_row(u)
        hp = unit_pair(u)
        use = use_mask[r]
        use_low = use.astype(BF)
        d_out = db_s[u].astype(F32)
        norms = []
        for a in range(2):
            far = far_s[a, u]
            inverse = 1.0 / den_s[a, u]
            product = d_out * far
            row = a * PAIRS + hp
            gb_s[pl.ds(row, 1), :] += jnp.sum(product, 0, keepdims=True)
            weight = blend_lanes(a, u)
            product = product * weight
            high = product.astype(BF)
            rest = (product - high.astype(F32)).astype(BF)
            dden = -(nn(high, ones_block) + nn(rest, ones_block)) * inverse
            dden_s[a, u] = dden
            dnum = (weight * d_out * inverse).astype(BF)
            low_s[a, u] = dnum
            used = fq_s[a, u] * use_low
            pay_s[1, u, a * E : (a + 1) * E, :] = pick(tn(used, dnum)).astype(BF)
            norm = jnp.sum(used.astype(F32) * dden, 0, keepdims=True)
            norms.append(jnp.broadcast_to(norm, (8, T)))
        pay_s[1, u, 2 * E : PAY, :] = jnp.concatenate(norms, 0).astype(BF)
        return 0

    lax.fori_loop(0, U, far_prepare, 0)
    chain_begin(1)

    def near_back(u, _):
        keys = two_blocks(k_s[u])
        halo_keys = two_blocks(hk_s[u])
        queries = q_s[u]
        d_out = db_s[u]
        dp = nt(d_out, two_blocks(v_s[u]))
        dp_halo = nt(d_out[:HALO], two_blocks(hv_s[u]))
        p = p_s[u]
        p_halo = ph_s[u]
        ds = []
        ds_halo = []
        for side in range(2):
            lanes = slice(side * T, (side + 1) * T)
            ps, phs = p[:, lanes], p_halo[:, lanes]
            delta = jnp.sum(ps * dp[:, lanes], -1, keepdims=True)
            delta_halo = delta[:HALO] + jnp.sum(phs * dp_halo[:, lanes], -1, keepdims=True)
            delta = jnp.concatenate([delta_halo, delta[HALO:]], 0)
            ds.append(ps * (dp[:, lanes] - delta))
            ds_halo.append(phs * (dp_halo[:, lanes] - delta_halo))
        ds = jnp.concatenate(ds, 1).astype(BF)
        ds_halo = jnp.concatenate(ds_halo, 1).astype(BF)
        dq_s[u] = nn(ds, keys) * SCALE
        dq_s[u, :HALO, :] += nn(ds_halo, halo_keys) * SCALE
        dk_s[u] = pick(tn(ds, queries)) * SCALE
        dv_s[u] = pick(tn(p.astype(BF), d_out))
        hdk_s[u] = (pick(tn(ds_halo, queries[:HALO])) * SCALE)[T - HALO :].astype(BF)
        hdv_s[u] = pick(tn(p_halo.astype(BF), d_out[:HALO]))[T - HALO :].astype(BF)
        return 0

    lax.fori_loop(0, U, near_back, 0)

    def halo_back(which, to):
        src, dst = ((hdk_s, hdk_r), (hdv_s, hdv_r))[which]
        return send(src, dst, halo_send.at[2 + which], halo_recv.at[2 + which], to)

    @pl.when(sq > 0)
    def _():
        for which in range(2):
            halo_back(which, sq - 1).start()

    chain_pair(1)

    def far_back(u, _):
        r = unit_row(u)
        values = two_blocks(v_s[u])
        mask = far_mask[r]
        mask = jnp.concatenate([mask, mask], 1)
        use = use_mask[r]
        queries = q_s[u].astype(F32)
        keys = k_s[u].astype(F32)
        dq = dq_s[u]
        dk = dk_s[u]
        dv = dv_s[u]
        for a, (_feature, slope) in enumerate(FEATURES):
            dnum = low_s[a, u]
            dden = dden_s[a, u]
            fq = fq_s[a, u]
            fk = two_blocks(fk_s[a, u])
            added = jnp.concatenate(
                [
                    jnp.broadcast_to(dden[:, 0:1], (T, T)),
                    jnp.broadcast_to(dden[:, E : E + 1], (T, T)),
                ],
                1,
            )
            d_kernel = ((nt(dnum, values) + added) * mask).astype(BF)
            dv += pick(tn(kk_s[a, u], dnum))
            state = two_blocks(in_s[0, u, a * E : (a + 1) * E, :])
            norm = in_s[0, u, 2 * E + 8 * a : 2 * E + 8 * a + 1, :].astype(F32)
            dfq = nn(d_kernel, fk) + use * (nt(dnum, state) + dden * norm)
            dq += dfq * slope(queries)
            dk += pick(tn(d_kernel, fq)) * slope(keys)
        dq_s[u] = dq
        dk_s[u] = dk
        dv_s[u] = dv
        return 0

    cut_back = (nz - 1 - z) * U // nz
    lax.fori_loop(0, cut_back, far_back, 0)
    chain_pass(1)
    lax.fori_loop(cut_back, U, far_back, 0)

    @pl.when(sq + 1 < n)
    def _():
        for which in range(2):
            halo_back(which, sq).wait_recv()

    chain_finish(1)

    def far_close(u, _):
        r = unit_row(u)
        hp = unit_pair(u)
        tail = tail_mask[r]
        keys = k_s[u].astype(F32)
        values = v_s[u]
        dk = dk_s[u]
        dv = dv_s[u]
        for a, (_feature, slope) in enumerate(FEATURES):
            state = two_blocks(in_s[1, u, a * E : (a + 1) * E, :])
            norm = in_s[1, u, 2 * E + 8 * a : 2 * E + 8 * a + 1, :].astype(F32)
            dk += tail * (nt(values, state) + norm) * slope(keys)
            dv += tail * nn(fk_s[a, u], state)
        zero = jnp.zeros((T - HALO, T), F32)
        dk += jnp.concatenate([zero, hdk_r[u].astype(F32)], 0)
        dv += jnp.concatenate([zero, hdv_r[u].astype(F32)], 0)
        rows = pl.ds(pl.multiple_of(r * T, T), T)
        lanes = pl.ds(pl.multiple_of(hp * T, T), T)
        wide_s[0, rows, lanes] = dq_s[u].astype(BF)
        wide_s[1, rows, lanes] = dk.astype(BF)
        wide_s[2, rows, lanes] = dv.astype(BF)
        return 0

    lax.fori_loop(0, U, far_close, 0)

    for i, weight in enumerate((w_query, w_key, w_value)):
        grads[ROW_Q + i * D : ROW_Q + (i + 1) * D, :] = tn(normed[...], wide_s[i]).astype(BF)
        back = nt(wide_s[i], weight[...])
        if i == 0:
            back_two[...] = back
        else:
            back_two[...] += back
    gain_grad_one = jnp.zeros((1, D), F32)
    for r in range(R):
        rows = pl.ds(r * T, T)
        x = tok[rows, :].astype(F32)
        inverse = lax.rsqrt(jnp.mean(x * x, -1, keepdims=True) + EPSILON)
        d_n = back_two[rows, :]
        gain_grad_one += jnp.sum(d_n * x * inverse, 0, keepdims=True)
        scaled = d_n * gain_one[...]
        d_x = (
            total[rows, :]
            + inverse * scaled
            - x * (inverse * inverse * inverse) * jnp.mean(x * scaled, -1, keepdims=True)
        )
        grad_tok[rows, :] = d_x.astype(BF)
    blends = [
        jnp.concatenate([gb_s[a * PAIRS + hp : a * PAIRS + hp + 1, :] for hp in range(PAIRS)], 1)
        for a in range(2)
    ]
    small = jnp.concatenate(
        [gain_grad_one, gain_grad_two] + blends + [jnp.zeros((SMALL - 4, D), F32)], 0
    )
    grads[ROW_SMALL:ROWS_ALL, :] = small.astype(BF)

    for slot, step in enumerate((1, 2, -1)):

        @pl.when((sq + step >= 0) & (sq + step < n))
        def _():
            info_copy(slot, sq + step).wait_send()

    @pl.when(sq + 1 < n)
    def _():
        for which in range(2):
            halo_copy(which, sq + 1).wait_send()

    @pl.when(sq > 0)
    def _():
        for which in range(2):
            halo_back(which, sq - 1).wait_send()

    chain_drain(0)
    chain_drain(1)


def solution(mesh):
    n = mesh.shape["seq"]

    def shards(
        tokens,
        segment_ids,
        padding,
        gain_one,
        w_query,
        w_key,
        w_value,
        blend,
        w_out,
        gain_two,
        w_up,
        w_down,
        cotangent,
    ):
        R, tok_count, _ = tokens.shape
        M = R * tok_count
        U = R * PAIRS
        HU = U // 2
        vmem = pl.BlockSpec(memory_space=pltpu.VMEM)
        anyspace = pl.BlockSpec(memory_space=pl.ANY)
        smem = pl.BlockSpec(memory_space=pltpu.SMEM)
        V = pltpu.VMEM
        unit_f = V((U, T, T), F32)
        unit_b = V((U, T, T), BF)
        two_f = V((2, U, T, T), F32)
        two_b = V((2, U, T, T), BF)
        wide_f = V((M, D), F32)
        wide_b = V((M, D), BF)
        halo_b = V((U, HALO, T), BF)
        dma = pltpu.SemaphoreType.DMA
        scratch = [
            V((D, D), BF),
            V((D, FF), BF),
            V((FF, D), BF),
            wide_b,
            wide_b,
            wide_b,
            wide_b,
            wide_f,
            wide_f,
            wide_f,
            unit_b,
            unit_b,
            unit_b,
            unit_b,
            unit_b,
            two_b,
            two_b,
            V((2, U, T, 2 * T), BF),
            V((U, T, 2 * T), F32),
            V((U, HALO, 2 * T), F32),
            unit_f,
            two_f,
            two_f,
            unit_b,
            two_b,
            two_f,
            unit_f,
            unit_f,
            unit_f,
            halo_b,
            halo_b,
            halo_b,
            halo_b,
            V((3, M, D), BF),
            V((R, T, T), F32),
            V((R, T, T), F32),
            V((R, T, T), F32),
            V((R, T, T), F32),
            V((R, HALO, T), F32),
            V((2, 8, T), F32),
            V((3, 2, 8, T), F32),
            V((2 * PAIRS, T), F32),
            V((2, U, PAY, T), BF),
            V((2, HU, PAY, T), BF),
            V((HU, PAY, T), F32),
            V((2, HU, PAY, T), BF),
            V((2, HU, PAY, T), BF),
            V((2, U, PAY, T), BF),
            V((2, HU, PAY, T), BF),
            dma((4,)),
            dma((3,)),
            dma((3,)),
            dma((4,)),
            dma((4,)),
            dma((2, 3, R)),
            dma((2, 3, R)),
        ]
        out, grad_tok, grads = pl.pallas_call(
            functools.partial(layer_kernel, n, R),
            out_shape=(
                jax.ShapeDtypeStruct((M, D), BF),
                jax.ShapeDtypeStruct((M, D), BF),
                jax.ShapeDtypeStruct((ROWS_ALL, D), BF),
            ),
            in_specs=[vmem] * 5 + [smem] + [vmem] * 3 + [anyspace] * 4,
            out_specs=(vmem, vmem, vmem),
            scratch_shapes=scratch,
            compiler_params=pltpu.CompilerParams(
                collective_id=0, has_side_effects=True, vmem_limit_bytes=60 * 1024 * 1024
            ),
            name="layer",
        )(
            tokens.reshape(M, D),
            segment_ids,
            padding,
            gain_one.reshape(1, D),
            gain_two.reshape(1, D),
            blend,
            w_query,
            w_key,
            w_value,
            w_out,
            w_up,
            w_down,
            cotangent.reshape(M, D),
        )
        grads = lax.psum(grads, ("seq", "rows")).astype(F32)
        small = grads[ROW_SMALL:]
        grad_up = jnp.concatenate(
            [grads[ROW_UP + t * D : ROW_UP + (t + 1) * D] for t in range(FF // D)], 1
        )
        return (
            out.reshape(R, tok_count, D),
            grad_tok.reshape(R, tok_count, D),
            small[0],
            grads[ROW_Q : ROW_Q + D],
            grads[ROW_Q + D : ROW_Q + 2 * D],
            grads[ROW_Q + 2 * D : ROW_Q + 3 * D],
            small[2:4].reshape(2, H, E).sum(-1),
            grads[ROW_OUT : ROW_OUT + D],
            small[1],
            grad_up,
            grads[:FF],
        )

    row, whole = P("rows", "seq", None), P()
    return jax.shard_map(
        shards,
        mesh=mesh,
        in_specs=(row, P("rows", "seq"), P("rows", "seq")) + (whole,) * 9 + (row,),
        out_specs=(row, row) + (whole,) * 9,
        check_vma=False,
    )
```

time: 624 us -> 266 us (0.43); the launches traced: 613 us -> 265 us
  blocking collectives: 179 us -> 0 us
  matrix products: 80.4 us -> 0 us
  Pallas kernels: 0 us -> 76.7 us
  waiting for transfers between devices: 224 us -> 159 us
  other arithmetic: 53.2 us -> 3.16 us
  local copies, waits for them, and re-layouts: 44.9 us -> 12.2 us
  starting transfers between devices: 14.3 us -> 0.04 us
    all_gather x4 -> x0, blocking collectives: 112 us -> none  [the longest x2 62.8 us: prefix_2(): lax.all_gather(a.astype(kind), axis)]
    dot_general x52 -> x0, matrix products: 80.4 us -> none  [the longest x2 5.1 us: far_back(): jnp.einsum('rqhf,rhef->rqhe', grad_numer, state_in, precision=EXACT_PRECI...]
    pallas_call x0 -> x1, Pallas kernels: none -> 76.7 us  [shards(): pl.pallas_call(functools.partial(layer_kernel, n, R), out_shape=(jax.Shap...]
    all_gather x4 -> x0, waiting for transfers between devices: 40.3 us -> none  [the longest x2 26.7 us: prefix_2(): lax.all_gather(a.astype(kind), axis)]
    psum x1 -> x0, blocking collectives: 39.6 us -> none  [shards(): lax.psum((grad_query, grad_key, grad_value, grad_out, grad_gain_one, grad...]
    select_n x45 -> x0, other arithmetic: 37 us -> none  [the longest x24 24.2 us: turn(): return jax.tree.map(lambda a, b: jnp.where(reached, a, b), new, before)]
    unnamed x1 -> x0, blocking collectives: 27.9 us -> none
    psum x1, waiting for transfers between devices: 184 us -> 159 us  [shards(): grads = lax.psum(grads, ('seq', 'rows')).astype(F32)]
  transfers between devices with their start and end apart: 10 -> 1, of which waited for: 3 -> 1; matrix products, arithmetic and copies ran while one was open for 18% -> 0% of each run, Pallas kernels for 0% -> 0%
where the time goes in v1:
time: 266 us; the launch traced here: 265 us
  waiting for transfers between devices  159 us (60%)
  Pallas kernels  76.7 us (29%)
  between operations  14.1 us (5%)
  local copies, waits for them, and re-layouts  12.2 us (5%)
  other arithmetic  3.16 us (1%)
    psum x1, waiting for transfers between devices, shards(): grads = lax.psum(grads, ('seq', 'rows')).astype(F32)  159 us
    pallas_call x1, Pallas kernels, shards(): pl.pallas_call(functools.partial(layer_kernel, n, R), out_shape=(jax.Shap...  76.7 us
  transfers between devices with their start and end apart: 1, of which 1 were waited for; matrix products, arithmetic and copies ran while one was open for 0% of the time, Pallas kernels for 0%

profile of v1, /device:TPU:1, one launch (start us, length us, event | category | flops | bytes accessed | tf_op | source)
XLA Modules:
  0.0 265.0 jit_solution(6122560761537327256)
XLA Ops:
  7.2 0.0 all-reduce.2.cloned.1.call-start
  7.2 76.7 %layer.1 = (bf16[384,512]{1,0:T(8,128)(2,1)}, bf16[384,512]{1,0:T(8,128)(2,1)}, bf16[6160,512]{1,0:T(8,128)(2,1)}) custom-call(bf16[384,512]{1,0:T(8,128)(2,1)} %bitcast.8, s32[3,128]{1,0:T(4,128)} %seg.1, s32[3,128]{1,0:T(4,128)} %pad.9, f32[1,512]{1,0:T(1,128)} %bitcast.12, f32[1,512]{1,0:T(1,128)} %bitcast.13, f32[2,8]{1,0:T(2,128)} %blend.1, ...), custom_call_target="tpu_custom_call" | custom-call | tf_op jit(solution)/shard_map/layer/pallas_call | solution.py:860
  83.9 0.0 all-reduce.2.cloned.1.call-update
  83.9 158.8 %all-reduce.2.cloned.1.call-done = bf16[6160,512]{1,0:T(8,128)(2,1)} async-done(((bf16[6160,512]{1,0:T(8,128)(2,1)}), bf16[6160,512]{1,0:T(8,128)(2,1)}) %all-reduce.2.cloned.1.call-update) | async-done | bytes 6307856 | tf_op jit(solution)/shard_map/psum | solution.py:889
  242.7 0.7 slice.56
  243.4 0.1 reshape.49
  243.5 0.7 reduce_sum.9
  244.1 5.0 %fusion = (f32[512,512]{1,0:T(8,128)S(1)}, f32[512,512]{1,0:T(8,128)S(1)}, f32[512,512]{1,0:T(8,128)S(1)}, f32[512,512]{1,0:T(8,128)S(1)}, f32[512,512]{1,0:T(8,...) fusion(bf16[6160,512]{1,0:T(8,128)(2,1)} %all-reduce.2.cloned.1.call-done), kind=kLoop, calls=%fused_computation.1 | loop fusion | bytes 16777216 | tf_op jit(solution)/shard_map/slice | solution.py:892
  249.1 0.0 copy-start
  249.1 2.5 pad_maximum_fusion
  251.6 1.8 copy-done
  253.4 0.6 fusion.1
  254.0 0.0 copy-start.2
  254.0 0.0 copy-start.1
  254.0 2.6 slice.63
  256.6 0.0 copy-done.2
  256.6 0.7 copy.27
  257.4 0.0 copy-done.1
  257.4 0.7 copy.28
Async XLA Ops:
  7.2 235.5 %all-reduce.2.cloned.1.call-start = ((), (), s32[]{:S(2)}) async-start(), calls=%async_computation | async-start | bytes 12615680 | tf_op jit(solution)/shard_map/psum | solution.py:889
  249.1 4.3 %copy-start = (bf16[6160,512]{1,0:T(8,128)(2,1)S(1)}, bf16[6160,512]{1,0:T(8,128)(2,1)}, u32[]{:S(2)}) copy-start(bf16[6160,512]{1,0:T(8,128)(2,1)} %all-reduce.2.cloned.1.call-done) | copy-start | bytes 18923524
  254.0 2.6 copy-start.2
  254.0 3.4 %copy-start.1 = (bf16[384,512]{1,0:T(8,128)(2,1)S(1)}, bf16[384,512]{1,0:T(8,128)(2,1)}, u32[]{:S(2)}) copy-start(bf16[384,512]{1,0:T(8,128)(2,1)} %get-tuple-element.15) | copy-start | bytes 1179652
Sparse Core Ops, SparseCore 0:
  84.1 158.5 all-reduce.1

commit v2 on v1

--- a/solution.py
+++ b/solution.py
@@ -25,12 +25,49 @@
 SCALE = 1.0 / math.sqrt(E)
 GELU_A = math.sqrt(2.0 / math.pi)
 GELU_B = 0.044715
-ROW_UP = FF
+TILES = FF // D
 ROW_OUT = 2 * FF
 ROW_Q = ROW_OUT + D
-ROW_SMALL = ROW_Q + 3 * D
-SMALL = 16
-ROWS_ALL = ROW_SMALL + SMALL
+ROWS_ALL = ROW_Q + 3 * D
+SMALL = 8
+LANES = D // 2
+CHUNKS = ((0, FF), (FF, FF), (ROW_OUT, 2 * D), (ROW_Q + D, 2 * D))
+PARTS = 4
+LAYER_VMEM = 60 * 1024 * 1024
+WIDEN_VMEM = 60 * 1024 * 1024
+
+
+def both(*steps):
+    return tuple((chunk, color, k) for chunk, k in steps for color in range(2))
+
+
+ORDER = {
+    "down": both((0, 0)),
+    "up": both((0, 1), (1, 0)),
+    "branch": both((1, 1)),
+    "prepare": both(),
+    "near_a": both(),
+    "near_b": both((0, 2)),
+    "pair": both((1, 2)),
+    "far_0": both(),
+    "far_1": both((0, 3)),
+    "far_2": both((1, 3)),
+    "far_3": both(),
+    "query": both((2, 0)),
+    "state": both((2, 1), (0, 4)),
+    "close": both((1, 4)),
+    "key": both((3, 0)),
+    "back": both((0, 5), (2, 2), (3, 1)),
+    "tail": both((1, 5), (3, 2), (0, 6), (2, 3), (3, 3), (1, 6), (2, 4), (3, 4), (0, 7), (2, 5), (3, 5), (1, 7), (0, 8), (2, 6), (3, 6), (1, 8), (2, 7), (3, 7), (2, 8), (3, 8)),
+}
+
+
+def row_down(t):
+    return (t // 2) * FF + (t % 2) * D
+
+
+def row_up(t):
+    return row_down(t) + FF // 2
 
 
 def nn(a, b):
@@ -91,9 +128,75 @@
 FEATURES = ((feature_one, slope_one), (feature_two, slope_two))
 
 
+def bits(size):
+    return size.bit_length() - 1
+
+
+def sum_order(color, n_rows, n_seq):
+    rows = [("rows", 2**b, 2) for b in range(bits(n_rows))]
+    seq = [("seq", 2**b, 2) for b in range(bits(n_seq))]
+    last = []
+    if len(seq) > 2:
+        last = [("seq", seq[-2][1], 4)]
+        seq = seq[:-2]
+    if color == 0:
+        return rows + seq + last
+    return rows[:1] + seq + rows[1:] + last
+
+
+def sum_plan(color, n_rows, n_seq, rows, offset):
+    plan = []
+    for axis, low, group in sum_order(color, n_rows, n_seq):
+        steps = [(low, group)]
+        if group == 4 and rows % 64:
+            steps = [(low, 2), (2 * low, 2)]
+        for low, group in steps:
+            split = rows % (16 * group) == 0
+            part = rows // group if split else rows
+            plan.append((axis, low, group, split, rows, part, offset))
+            offset += (group - 1) * part
+            rows = part
+    return plan, offset
+
+
+def sum_plans(n_rows, n_seq):
+    plans = []
+    offset = [0, 0]
+    for _base, rows in CHUNKS:
+        both = []
+        for color in range(2):
+            plan, offset[color] = sum_plan(color, n_rows, n_seq, rows, offset[color])
+            both.append(plan)
+        plans.append(both)
+    return plans, max(offset)
+
+
 def layer_kernel(
     n,
+    n_rows,
     R,
+    tok_hbm,
+    seg_hbm,
+    pad_hbm,
+    gain_one_hbm,
+    gain_two_hbm,
+    blend_hbm,
+    w_query_hbm,
+    w_key_hbm,
+    w_value_hbm,
+    w_out_hbm,
+    w_up_hbm,
+    w_down_hbm,
+    cot_hbm,
+    out,
+    grad_tok,
+    small_out,
+    full_hbm,
+    grads,
+    full,
+    landed,
+    small_s,
+    small_r,
     tok,
     seg,
     pad,
@@ -103,17 +206,11 @@
     w_query,
     w_key,
     w_value,
-    w_out_hbm,
-    w_up_hbm,
-    w_down_hbm,
-    cot_hbm,
-    out,
-    grad_tok,
-    grads,
     w_out,
     w_up,
     w_down,
     cot,
+    weight_s,
     normed,
     normed_two,
     mixed,
@@ -136,7 +233,6 @@
     db_s,
     low_s,
     dden_s,
-    dq_s,
     dk_s,
     dv_s,
     hdk_s,
@@ -166,6 +262,11 @@
     halo_recv,
     chain_send,
     chain_recv,
+    sum_send,
+    sum_recv,
+    small_send,
+    small_recv,
+    full_sem,
 ):
     U = R * PAIRS
     HU = U // 2
@@ -206,25 +307,68 @@
         def _():
             pl.semaphore_signal(barrier, inc=1, device_id=(sq + step, rw), device_id_type=MESH)
 
+    plans, _size = sum_plans(n_rows, n)
+    partners = [("rows", 2**b) for b in range(bits(n_rows))]
+    partners += [("seq", 2**b) for b in range(bits(n))]
+
+    def peer_of(axis, low, group, step):
+        own = rw if axis == "rows" else sq
+        mine = lax.rem(own // low, group)
+        other = own + (lax.rem(mine + step, group) - mine) * low
+        return mine, ((sq, other) if axis == "rows" else (other, rw))
+
+    groups = {(axis, low, 2) for axis, low in partners}
+    for both in plans:
+        for plan in both:
+            groups |= {(axis, low, group) for axis, low, group, *_ in plan}
+    greet = [(axis, low, group, d) for axis, low, group in sorted(groups) for d in range(1, group)]
+    for axis, low, group, d in greet:
+        pl.semaphore_signal(
+            barrier, inc=1, device_id=peer_of(axis, low, group, d)[1], device_id_type=MESH
+        )
+
     loads = [
         pltpu.make_async_copy(src, dst, w_sem.at[i])
         for i, (src, dst) in enumerate(
-            ((w_out_hbm, w_out), (w_up_hbm, w_up), (w_down_hbm, w_down), (cot_hbm, cot))
+            (
+                (tok_hbm, tok),
+                (gain_one_hbm, gain_one),
+                (w_key_hbm, w_key),
+                (w_value_hbm, w_value),
+                (seg_hbm, seg),
+                (pad_hbm, pad),
+                (w_query_hbm, w_query),
+                (blend_hbm, blend),
+                (gain_two_hbm, gain_two),
+                (w_out_hbm, w_out),
+                (w_up_hbm, w_up),
+                (w_down_hbm, w_down),
+                (cot_hbm, cot),
+            )
         )
     ]
     for load in loads:
         load.start()
+    loads[0].wait()
+    loads[1].wait()
 
     for r in range(R):
         rows = pl.ds(r * T, T)
         x = tok[rows, :].astype(F32)
         inverse = lax.rsqrt(jnp.mean(x * x, -1, keepdims=True) + EPSILON)
         normed[rows, :] = (x * inverse * gain_one[...]).astype(BF)
-    for weight, held in ((w_key, k_s), (w_value, v_s), (w_query, q_s)):
+
+    def project(load, weight, held):
+        loads[load].wait()
         whole = nn(normed[...], weight[...]).astype(BF)
         for r in range(R):
             for hp in range(PAIRS):
                 held[unit_of(r, hp)] = whole[r * T : (r + 1) * T, hp * T : (hp + 1) * T]
+
+    project(2, w_key, k_s)
+    project(3, w_value, v_s)
+    loads[4].wait()
+    loads[5].wait()
 
     i_pos = lax.broadcasted_iota(jnp.int32, (T, T), 0)
     j_pos = lax.broadcasted_iota(jnp.int32, (T, T), 1)
@@ -261,36 +405,6 @@
         hdk_r[...] = jnp.zeros((U, HALO, T), BF)
         hdv_r[...] = jnp.zeros((U, HALO, T), BF)
 
-    pl.semaphore_wait(barrier, jnp.minimum(sq, 2) + jnp.minimum(n - 1 - sq, 2))
-
-    def info_copy(slot, to):
-        return send(info_own, info_in.at[slot], info_send.at[slot], info_recv.at[slot], to)
-
-    def halo_copy(which, to):
-        src, dst = ((k_s, hk_s), (v_s, hv_s))[which]
-        tail = pl.ds(T - HALO, HALO)
-        return send(
-            src.at[:, tail, :], dst.at[:, tail, :], halo_send.at[which], halo_recv.at[which], to
-        )
-
-    for slot, step in enumerate((1, 2, -1)):
-        inside = (sq + step >= 0) & (sq + step < n)
-        came = (sq - step >= 0) & (sq - step < n)
-
-        @pl.when(inside)
-        def _():
-            info_copy(slot, sq + step).start()
-
-        @pl.when(jnp.logical_not(came))
-        def _():
-            info_in[slot, 0] = jnp.full((8, T), -1.0, F32)
-            info_in[slot, 1] = jnp.zeros((8, T), F32)
-
-    @pl.when(sq + 1 < n)
-    def _():
-        for which in range(2):
-            halo_copy(which, sq + 1).start()
-
     ones_block = block_ones()
 
     def local_state(u, _):
@@ -311,6 +425,179 @@
 
     lax.fori_loop(0, U, local_state, 0)
 
+    pl.semaphore_wait(barrier, jnp.minimum(sq, 2) + jnp.minimum(n - 1 - sq, 2) + len(greet))
+
+    def starts_of(chunk, color):
+        start = CHUNKS[chunk][0]
+        found = [start]
+        for axis, low, group, split, _rows, part, _offset in plans[chunk][color]:
+            if split:
+                start = start + peer_of(axis, low, group, 1)[0] * part
+            found.append(start)
+        return found
+
+    starts = [[starts_of(c, color) for color in range(2)] for c in range(len(CHUNKS))]
+
+    def aligned(start, size):
+        return pl.ds(pl.multiple_of(start, 16), size)
+
+    def sum_copy(src, dst, chunk, color, slot, d, to):
+        return pltpu.make_async_remote_copy(
+            src_ref=src,
+            dst_ref=dst,
+            send_sem=sum_send.at[chunk, color, slot, d - 1],
+            recv_sem=sum_recv.at[chunk, color, slot, d - 1],
+            device_id=to,
+            device_id_type=MESH,
+        )
+
+    def scatter_copy(chunk, color, k, d):
+        axis, low, group, split, _rows, part, offset = plans[chunk][color][k]
+        mine, to = peer_of(axis, low, group, d)
+        start = starts[chunk][color][k]
+        if split:
+            start = start + lax.rem(mine + d, group) * part
+        src = grads.at[color, aligned(start, part)]
+        dst = landed.at[color, pl.ds(offset + (d - 1) * part, part)]
+        return sum_copy(src, dst, chunk, color, k, d, to)
+
+    def scatter_add(chunk, color, k):
+        axis, low, group, split, _rows, part, offset = plans[chunk][color][k]
+        for d in range(1, group):
+            scatter_copy(chunk, color, k, d).wait_recv()
+        if not split:
+            scatter_copy(chunk, color, k, 1).wait_send()
+        start = starts[chunk][color][k + 1]
+        block = math.gcd(part, 128)
+        target = full if k + 1 == len(plans[chunk][color]) else grads
+
+        def add(i, _):
+            here = aligned(start + i * block, block)
+            value = grads[color, here, :]
+            for d in range(1, group):
+                at = pl.multiple_of(offset + (d - 1) * part + i * block, 16)
+                value += landed[color, pl.ds(at, block), :]
+            target[color, here, :] = value
+            return 0
+
+        lax.fori_loop(0, part // block, add, 0)
+
+    def gather_copy(chunk, color, k, d):
+        axis, low, group, _split, _rows, part, _offset = plans[chunk][color][k]
+        here = full.at[color, aligned(starts[chunk][color][k + 1], part)]
+        slot = 2 * len(plans[chunk][color]) - 1 - k
+        return sum_copy(here, here, chunk, color, slot, d, peer_of(axis, low, group, d)[1])
+
+    def gather_arrival(chunk, color, k):
+        axis, low, group, _split, _rows, part, _offset = plans[chunk][color][k]
+        slot = 2 * len(plans[chunk][color]) - 1 - k
+        for d in range(1, group):
+            mine, to = peer_of(axis, low, group, d)
+            source = lax.rem(mine - d + group, group)
+            here = full.at[color, aligned(starts[chunk][color][k] + source * part, part)]
+            sum_copy(here, here, chunk, color, slot, d, to).wait_recv()
+
+    def sum_step(chunk, color, k):
+        plan = plans[chunk][color]
+        K = len(plan)
+        if 1 <= k <= K:
+            scatter_add(chunk, color, k - 1)
+        elif K < k <= 2 * K and plan[2 * K - k][3]:
+            gather_arrival(chunk, color, 2 * K - k)
+        if k < K:
+            for d in range(1, plan[k][2]):
+                scatter_copy(chunk, color, k, d).start()
+        elif k < 2 * K and plan[2 * K - 1 - k][3]:
+            for d in range(1, plan[2 * K - 1 - k][2]):
+                gather_copy(chunk, color, 2 * K - 1 - k, d).start()
+
+    def full_copy(chunk, color):
+        base, rows = CHUNKS[chunk]
+        here = pl.ds(base, rows)
+        return pltpu.make_async_copy(
+            full.at[color, here], full_hbm.at[color, here], full_sem.at[chunk, color]
+        )
+
+    done = {}
+
+    def sums(steps):
+        for chunk, color, k in steps:
+            last = 2 * len(plans[chunk][color])
+            at = done.get((chunk, color), 0)
+            while at <= min(k, last):
+                sum_step(chunk, color, at)
+                at += 1
+                if at > last:
+                    full_copy(chunk, color).start()
+            done[chunk, color] = at
+
+    def sums_rest():
+        while True:
+            left = [
+                (chunk, color, done.get((chunk, color), 0))
+                for chunk in range(len(CHUNKS))
+                for color in range(2)
+                if done.get((chunk, color), 0) <= 2 * len(plans[chunk][color])
+            ]
+            if not left:
+                return
+            sums(left)
+
+    def sum_drain(chunk):
+        for color in range(2):
+            for k, stage in enumerate(plans[chunk][color]):
+                for d in range(1, stage[2]):
+                    if stage[3]:
+                        scatter_copy(chunk, color, k, d).wait_send()
+                        gather_copy(chunk, color, k, d).wait_send()
+
+    def small_copy(b):
+        axis, low = partners[b]
+        return pltpu.make_async_remote_copy(
+            src_ref=small_s,
+            dst_ref=small_r.at[b],
+            send_sem=small_send.at[b],
+            recv_sem=small_recv.at[b],
+            device_id=peer_of(axis, low, 2, 1)[1],
+            device_id_type=MESH,
+        )
+
+    def small_step(b):
+        if 1 <= b <= len(partners):
+            small_copy(b - 1).wait()
+            small_s[...] += small_r[b - 1]
+        if b < len(partners):
+            small_copy(b).start()
+
+    def keep(base, value):
+        low = value.astype(BF)
+        rows = pl.ds(base, value.shape[0])
+        grads[0, rows, :] = low[:, :LANES]
+        grads[1, rows, :] = low[:, LANES:]
+
+    def info_copy(slot, to):
+        return send(info_own, info_in.at[slot], info_send.at[slot], info_recv.at[slot], to)
+
+    def halo_copy(which, to):
+        src, dst = ((k_s, hk_s), (v_s, hv_s))[which]
+        tail = pl.ds(T - HALO, HALO)
+        return send(
+            src.at[:, tail, :], dst.at[:, tail, :], halo_send.at[which], halo_recv.at[which], to
+        )
+
+    for slot, step in enumerate((1, 2, -1)):
+        inside = (sq + step >= 0) & (sq + step < n)
+        came = (sq - step >= 0) & (sq - step < n)
+
+        @pl.when(inside)
+        def _():
+            info_copy(slot, sq + step).start()
+
+        @pl.when(jnp.logical_not(came))
+        def _():
+            info_in[slot, 0] = jnp.full((8, T), -1.0, F32)
+            info_in[slot, 1] = jnp.zeros((8, T), F32)
+
     def half(which, r):
         return pl.ds(which * HU + 2 * r, 2)
 
@@ -412,6 +699,21 @@
 
     chain_begin(0)
 
+    @pl.when(sq + 1 < n)
+    def _():
+        for which in range(2):
+            halo_copy(which, sq + 1).start()
+
+    project(6, w_query, q_s)
+    loads[7].wait()
+    loads[8].wait()
+    for a in range(2):
+        for hp in range(PAIRS):
+            sides = [
+                jnp.broadcast_to(blend[a : a + 1, 2 * hp + side : 2 * hp + side + 1], (1, T))
+                for side in range(2)
+            ]
+            weight_s[a * PAIRS + hp : a * PAIRS + hp + 1, :] = jnp.where(lane_low(1), *sides)
     ones_pair = two_blocks(jnp.ones((T, T), BF))
 
     def far_local(u, _):
@@ -486,9 +788,7 @@
     chain_finish(0)
 
     def blend_lanes(a, u):
-        hp = unit_pair(u)
-        low = lane_low(1)
-        return jnp.where(low, blend[a, 2 * hp], blend[a, 2 * hp + 1])
+        return weight_s[pl.ds(a * PAIRS + unit_pair(u), 1), :]
 
     def far_finish(u, _):
         r = unit_row(u)
@@ -513,7 +813,7 @@
 
     lax.fori_loop(0, U, far_finish, 0)
 
-    loads[0].wait()
+    loads[9].wait()
     middle[...] = tok[...].astype(F32) + nn(mixed[...], w_out[...])
     for r in range(R):
         rows = pl.ds(r * T, T)
@@ -522,12 +822,12 @@
         normed_two[rows, :] = (mid * inverse * gain_two[...]).astype(BF)
     total[...] = jnp.zeros_like(total)
     back_two[...] = jnp.zeros_like(back_two)
-    loads[1].wait()
-    loads[2].wait()
-    loads[3].wait()
+    for i in (10, 11, 12):
+        loads[i].wait()
 
     def feed(t, _):
-        cols = pl.ds(pl.multiple_of(t * D, D), D)
+        at = pl.multiple_of(t * D, D)
+        cols = pl.ds(at, D)
         up = nn(normed_two[...], w_up[:, cols])
         square = up * up
         tangent = jnp.tanh(GELU_A * (up + GELU_B * square * up))
@@ -536,14 +836,16 @@
             1.0 + 3.0 * GELU_B * square
         )
         total[...] += nn(act, w_down[cols, :])
-        g = cot[...]
-        grads[cols, :] = tn(act, g).astype(BF)
-        d_up = (nt(g, w_down[cols, :]) * slope).astype(BF)
-        grads[pl.ds(pl.multiple_of(ROW_UP + t * D, D), D), :] = tn(normed_two[...], d_up).astype(BF)
+        keep(pl.multiple_of(row_down(t), D), tn(act, cot[...]))
+        d_up = (nt(cot[...], w_down[cols, :]) * slope).astype(BF)
+        keep(pl.multiple_of(row_up(t), D), tn(normed_two[...], d_up))
         back_two[...] += nt(d_up, w_up[:, cols])
         return 0
 
-    lax.fori_loop(0, FF // D, feed, 0)
+    lax.fori_loop(0, TILES // 2, feed, 0)
+    sums(ORDER["down"])
+    lax.fori_loop(TILES // 2, TILES, feed, 0)
+    sums(ORDER["up"])
     out[...] = (middle[...] + total[...]).astype(BF)
 
     gain_grad_two = jnp.zeros((1, D), F32)
@@ -562,11 +864,12 @@
         total[rows, :] = d_mid
         normed_two[rows, :] = d_mid.astype(BF)
     d_branch = normed_two[...]
-    grads[ROW_OUT : ROW_OUT + D, :] = tn(mixed[...], d_branch).astype(BF)
+    keep(ROW_OUT, tn(mixed[...], d_branch))
     d_blended = nt(d_branch, w_out[...]).astype(BF)
     for r in range(R):
         for hp in range(PAIRS):
             db_s[unit_of(r, hp)] = d_blended[r * T : (r + 1) * T, hp * T : (hp + 1) * T]
+    sums(ORDER["branch"])
 
     gb_s[...] = jnp.zeros_like(gb_s)
 
@@ -622,15 +925,19 @@
             ds_halo.append(phs * (dp_halo[:, lanes] - delta_halo))
         ds = jnp.concatenate(ds, 1).astype(BF)
         ds_halo = jnp.concatenate(ds_halo, 1).astype(BF)
-        dq_s[u] = nn(ds, keys) * SCALE
-        dq_s[u, :HALO, :] += nn(ds_halo, halo_keys) * SCALE
+        near_s[u] = nn(ds, keys) * SCALE
+        near_s[u, :HALO, :] += nn(ds_halo, halo_keys) * SCALE
         dk_s[u] = pick(tn(ds, queries)) * SCALE
         dv_s[u] = pick(tn(p.astype(BF), d_out))
         hdk_s[u] = (pick(tn(ds_halo, queries[:HALO])) * SCALE)[T - HALO :].astype(BF)
         hdv_s[u] = pick(tn(p_halo.astype(BF), d_out[:HALO]))[T - HALO :].astype(BF)
         return 0
 
-    lax.fori_loop(0, U, near_back, 0)
+    sums(ORDER["prepare"])
+    lax.fori_loop(0, HU, near_back, 0)
+    sums(ORDER["near_a"])
+    lax.fori_loop(HU, U, near_back, 0)
+    sums(ORDER["near_b"])
 
     def halo_back(which, to):
         src, dst = ((hdk_s, hdk_r), (hdv_s, hdv_r))[which]
@@ -642,6 +949,7 @@
             halo_back(which, sq - 1).start()
 
     chain_pair(1)
+    sums(ORDER["pair"])
 
     def far_back(u, _):
         r = unit_row(u)
@@ -651,7 +959,7 @@
         use = use_mask[r]
         queries = q_s[u].astype(F32)
         keys = k_s[u].astype(F32)
-        dq = dq_s[u]
+        dq = near_s[u]
         dk = dk_s[u]
         dv = dv_s[u]
         for a, (_feature, slope) in enumerate(FEATURES):
@@ -673,15 +981,27 @@
             dfq = nn(d_kernel, fk) + use * (nt(dnum, state) + dden * norm)
             dq += dfq * slope(queries)
             dk += pick(tn(d_kernel, fq)) * slope(keys)
-        dq_s[u] = dq
+        near_s[u] = dq
         dk_s[u] = dk
         dv_s[u] = dv
         return 0
 
-    cut_back = (nz - 1 - z) * U // nz
-    lax.fori_loop(0, cut_back, far_back, 0)
-    chain_pass(1)
-    lax.fori_loop(cut_back, U, far_back, 0)
+    turn = (nz - 1 - z) * PARTS // nz
+    for part in range(PARTS):
+
+        @pl.when(turn == part)
+        def _():
+            chain_pass(1)
+
+        lax.fori_loop(part * U // PARTS, (part + 1) * U // PARTS, far_back, 0)
+        sums(ORDER["far_%d" % part])
+
+    for u in range(U):
+        r, hp = (u % (2 * R)) // 2, (u // (2 * R)) * 2 + u % 2
+        wide_s[0, r * T : (r + 1) * T, hp * T : (hp + 1) * T] = near_s[u].astype(BF)
+    keep(ROW_Q, tn(normed[...], wide_s[0]))
+    sums(ORDER["query"])
+    back_two[...] = nt(wide_s[0], w_query[...])
 
     @pl.when(sq + 1 < n)
     def _():
@@ -689,6 +1009,7 @@
             halo_back(which, sq).wait_recv()
 
     chain_finish(1)
+    sums(ORDER["state"])
 
     def far_close(u, _):
         r = unit_row(u)
@@ -708,20 +1029,17 @@
         dv += jnp.concatenate([zero, hdv_r[u].astype(F32)], 0)
         rows = pl.ds(pl.multiple_of(r * T, T), T)
         lanes = pl.ds(pl.multiple_of(hp * T, T), T)
-        wide_s[0, rows, lanes] = dq_s[u].astype(BF)
         wide_s[1, rows, lanes] = dk.astype(BF)
         wide_s[2, rows, lanes] = dv.astype(BF)
         return 0
 
     lax.fori_loop(0, U, far_close, 0)
-
-    for i, weight in enumerate((w_query, w_key, w_value)):
-        grads[ROW_Q + i * D : ROW_Q + (i + 1) * D, :] = tn(normed[...], wide_s[i]).astype(BF)
-        back = nt(wide_s[i], weight[...])
-        if i == 0:
-            back_two[...] = back
-        else:
-            back_two[...] += back
+    sums(ORDER["close"])
+    for i in (1, 2):
+        keep(ROW_Q + i * D, tn(normed[...], wide_s[i]))
+    sums(ORDER["key"])
+    for i, weight in ((1, w_key), (2, w_value)):
+        back_two[...] += nt(wide_s[i], weight[...])
     gain_grad_one = jnp.zeros((1, D), F32)
     for r in range(R):
         rows = pl.ds(r * T, T)
@@ -740,10 +1058,19 @@
         jnp.concatenate([gb_s[a * PAIRS + hp : a * PAIRS + hp + 1, :] for hp in range(PAIRS)], 1)
         for a in range(2)
     ]
-    small = jnp.concatenate(
+    small_s[...] = jnp.concatenate(
         [gain_grad_one, gain_grad_two] + blends + [jnp.zeros((SMALL - 4, D), F32)], 0
     )
-    grads[ROW_SMALL:ROWS_ALL, :] = small.astype(BF)
+    small_step(0)
+    sums(ORDER["back"])
+    for i, step in enumerate(ORDER["tail"]):
+        sums((step,))
+        if i % 2 and i // 2 < len(partners):
+            small_step(i // 2 + 1)
+    for b in range(len(ORDER["tail"]) // 2, len(partners)):
+        small_step(b + 1)
+    sums_rest()
+    small_out[...] = small_s[...]
 
     for slot, step in enumerate((1, 2, -1)):
 
@@ -763,10 +1090,75 @@
 
     chain_drain(0)
     chain_drain(1)
+    for c in range(len(CHUNKS)):
+        sum_drain(c)
+        for color in range(2):
+            full_copy(c, color).wait()
+
+
+def widen_kernel(
+    grads,
+    small,
+    out_in,
+    back_in,
+    g_one,
+    g_two,
+    g_blend,
+    g_query,
+    g_key,
+    g_value,
+    g_out,
+    g_up,
+    g_down,
+    out,
+    back,
+    held,
+    wide,
+    in_sem,
+    out_sem,
+    same_sem,
+):
+    blocks = ROWS_ALL // D
+    targets = []
+    for t in (0, 2):
+        targets += [g_down.at[pl.ds((t + i) * D, D)] for i in range(2)]
+        targets += [g_up.at[:, pl.ds((t + i) * D, D)] for i in range(2)]
+    targets += [g_out, g_query, g_key, g_value]
+    reads = [
+        pltpu.make_async_copy(grads.at[:, pl.ds(i * D, D)], held.at[i], in_sem.at[i])
+        for i in range(blocks)
+    ]
+    for read in reads:
+        read.start()
+    writes = [
+        pltpu.make_async_copy(wide.at[i], targets[i], out_sem.at[i]) for i in range(blocks)
+    ]
+    same = [
+        pltpu.make_async_copy(out_in, out, same_sem.at[0]),
+        pltpu.make_async_copy(back_in, back, same_sem.at[1]),
+    ]
+    for copy in same:
+        copy.start()
+    g_one[...] = small[0]
+    g_two[...] = small[1]
+    for a in range(2):
+        row = small[2 + a : 3 + a, :]
+        lane = lax.broadcasted_iota(jnp.int32, (H, D), 1) // E
+        head = lax.broadcasted_iota(jnp.int32, (H, D), 0)
+        per_head = jnp.sum(jnp.where(lane == head, row, 0.0), -1, keepdims=True)
+        g_blend[a : a + 1, :] = jnp.broadcast_to(per_head, (H, H)).T[:1]
+    for i in range(blocks):
+        reads[i].wait()
+        wide[i, :, :LANES] = held[i, 0].astype(F32)
+        wide[i, :, LANES:] = held[i, 1].astype(F32)
+        writes[i].start()
+    for copy in writes + same:
+        copy.wait()
 
 
 def solution(mesh):
     n = mesh.shape["seq"]
+    n_rows = mesh.shape["rows"]
 
     def shards(
         tokens,
@@ -789,7 +1181,6 @@
         HU = U // 2
         vmem = pl.BlockSpec(memory_space=pltpu.VMEM)
         anyspace = pl.BlockSpec(memory_space=pl.ANY)
-        smem = pl.BlockSpec(memory_space=pltpu.SMEM)
         V = pltpu.VMEM
         unit_f = V((U, T, T), F32)
         unit_b = V((U, T, T), BF)
@@ -799,11 +1190,29 @@
         wide_b = V((M, D), BF)
         halo_b = V((U, HALO, T), BF)
         dma = pltpu.SemaphoreType.DMA
+        plans, landed_rows = sum_plans(n_rows, n)
+        stages = 2 * max(len(plan) for both in plans for plan in both)
+        count = bits(n) + bits(n_rows)
         scratch = [
+            V((2, ROWS_ALL, LANES), BF),
+            V((2, ROWS_ALL, LANES), BF),
+            V((2, landed_rows, LANES), BF),
+            V((SMALL, D), F32),
+            V((count, SMALL, D), F32),
+            wide_b,
+            V((R, T), jnp.int32),
+            V((R, T), jnp.int32),
+            V((1, D), F32),
+            V((1, D), F32),
+            V((2, H), F32),
+            V((D, D), BF),
+            V((D, D), BF),
+            V((D, D), BF),
             V((D, D), BF),
             V((D, FF), BF),
             V((FF, D), BF),
             wide_b,
+            V((2 * PAIRS, T), F32),
             wide_b,
             wide_b,
             wide_b,
@@ -828,7 +1237,6 @@
             two_f,
             unit_f,
             unit_f,
-            unit_f,
             halo_b,
             halo_b,
             halo_b,
@@ -849,26 +1257,32 @@
             V((2, HU, PAY, T), BF),
             V((2, U, PAY, T), BF),
             V((2, HU, PAY, T), BF),
-            dma((4,)),
+            dma((13,)),
             dma((3,)),
             dma((3,)),
             dma((4,)),
             dma((4,)),
             dma((2, 3, R)),
             dma((2, 3, R)),
+            dma((len(CHUNKS), 2, stages, 3)),
+            dma((len(CHUNKS), 2, stages, 3)),
+            dma((count,)),
+            dma((count,)),
+            dma((len(CHUNKS), 2)),
         ]
-        out, grad_tok, grads = pl.pallas_call(
-            functools.partial(layer_kernel, n, R),
+        out, grad_tok, small, grads = pl.pallas_call(
+            functools.partial(layer_kernel, n, n_rows, R),
             out_shape=(
                 jax.ShapeDtypeStruct((M, D), BF),
                 jax.ShapeDtypeStruct((M, D), BF),
-                jax.ShapeDtypeStruct((ROWS_ALL, D), BF),
+                jax.ShapeDtypeStruct((SMALL, D), F32),
+                jax.ShapeDtypeStruct((2, ROWS_ALL, LANES), BF),
             ),
-            in_specs=[vmem] * 5 + [smem] + [vmem] * 3 + [anyspace] * 4,
-            out_specs=(vmem, vmem, vmem),
+            in_specs=[pl.BlockSpec(memory_space=pltpu.HBM)] * 13,
+            out_specs=(vmem, vmem, vmem, anyspace),
             scratch_shapes=scratch,
             compiler_params=pltpu.CompilerParams(
-                collective_id=0, has_side_effects=True, vmem_limit_bytes=60 * 1024 * 1024
+                collective_id=0, has_side_effects=True, vmem_limit_bytes=LAYER_VMEM
             ),
             name="layer",
         )(
@@ -886,23 +1300,49 @@
             w_down,
             cotangent.reshape(M, D),
         )
-        grads = lax.psum(grads, ("seq", "rows")).astype(F32)
-        small = grads[ROW_SMALL:]
-        grad_up = jnp.concatenate(
-            [grads[ROW_UP + t * D : ROW_UP + (t + 1) * D] for t in range(FF // D)], 1
-        )
+        square = jax.ShapeDtypeStruct((D, D), F32)
+        token = jax.ShapeDtypeStruct((M, D), BF)
+        blocks = ROWS_ALL // D
+        g_one, g_two, g_blend, g_query, g_key, g_value, g_out, g_up, g_down, out, grad_tok = (
+          pl.pallas_call(
+            widen_kernel,
+            out_shape=(
+                jax.ShapeDtypeStruct((D,), F32),
+                jax.ShapeDtypeStruct((D,), F32),
+                jax.ShapeDtypeStruct((2, H), F32),
+                square,
+                square,
+                square,
+                square,
+                jax.ShapeDtypeStruct((D, FF), F32),
+                jax.ShapeDtypeStruct((FF, D), F32),
+                token,
+                token,
+            ),
+            in_specs=[anyspace, vmem, vmem, vmem],
+            out_specs=(vmem,) * 3 + (anyspace,) * 8,
+            scratch_shapes=[
+                V((blocks, 2, D, LANES), BF),
+                V((blocks, D, D), F32),
+                dma((blocks,)),
+                dma((blocks,)),
+                dma((2,)),
+            ],
+            compiler_params=pltpu.CompilerParams(vmem_limit_bytes=WIDEN_VMEM),
+            name="widen",
+        )(grads, small, out, grad_tok))
         return (
             out.reshape(R, tok_count, D),
             grad_tok.reshape(R, tok_count, D),
-            small[0],
-            grads[ROW_Q : ROW_Q + D],
-            grads[ROW_Q + D : ROW_Q + 2 * D],
-            grads[ROW_Q + 2 * D : ROW_Q + 3 * D],
-            small[2:4].reshape(2, H, E).sum(-1),
-            grads[ROW_OUT : ROW_OUT + D],
-            small[1],
-            grad_up,
-            grads[:FF],
+            g_one,
+            g_query,
+            g_key,
+            g_value,
+            g_blend,
+            g_out,
+            g_two,
+            g_up,
+            g_down,
         )
 
     row, whole = P("rows", "seq", None), P()

time: 266 us -> 150 us (0.56)
  waiting for transfers between devices: 159 us -> 0 us
  Pallas kernels: 76.7 us -> 149 us
  between operations: 14.1 us -> 0.82 us
  local copies, waits for them, and re-layouts: 12.2 us -> 0 us
  other arithmetic: 3.16 us -> 0 us
    psum x1 -> x0, waiting for transfers between devices: 159 us -> none  [shards(): grads = lax.psum(grads, ('seq', 'rows')).astype(F32)]
    pallas_call x1 -> x2, Pallas kernels: 76.7 us -> 149 us  [the longest x1 141 us: shards(): pl.pallas_call(functools.partial(layer_kernel, n, n_rows, R), out_shape=(...]
    slice x4 -> x0, local copies, waits for them, and re-layouts: 8.87 us -> none  [the longest x1 4.98 us: shards(): grads[ROW_UP + t * D:ROW_UP + (t + 1) * D]]
    unnamed x8 -> x0, local copies, waits for them, and re-layouts: 3.29 us -> none
  transfers between devices with their start and end apart: 1 -> 0, of which waited for: 1 -> 0; matrix products, arithmetic and copies ran while one was open for 0% -> 0% of each run, Pallas kernels for 0% -> 0%
where the time goes in v2:
time: 150 us
  Pallas kernels  149 us (99%)
    pallas_call x1, Pallas kernels, shards(): pl.pallas_call(functools.partial(layer_kernel, n, n_rows, R), out_shape=(...  141 us
    pallas_call x1, Pallas kernels, shards(): pl.pallas_call(widen_kernel, out_shape=(jax.ShapeDtypeStruct((D,), F32),...  8.19 us

profile of v2, /device:TPU:1, one launch (start us, length us, event | category | flops | bytes accessed | tf_op | source)
XLA Modules:
  0.0 149.9 jit_solution(4432504667222675760)
XLA Ops:
  0.6 140.9 %layer.1 = (bf16[384,512]{1,0:T(8,128)(2,1)}, bf16[384,512]{1,0:T(8,128)(2,1)}, f32[8,512]{1,0:T(8,128)}, bf16[2,6144,256]{2,1,0:T(8,128)(2,1)}) custom-call(bf16[384,512]{1,0:T(8,128)(2,1)} %bitcast.6, s32[3,128]{1,0:T(4,128)} %seg_hbm.1, s32[3,128]{1,0:T(4,128)} %pad_hbm.1, f32[1,512]{1,0:T(1,128)} %bitcast.8, f32[1,512]{1,0:T(1,128)} %bitcast.9, ...), custom_call_target="tpu_custom_call" | custom-call | tf_op jit(solution)/shard_map/layer/pallas_call | solution.py:1273
  141.5 8.2 %widen.1 = (f32[512]{0:T(512)}, f32[512]{0:T(512)}, f32[2,8]{1,0:T(2,128)}, f32[512,512]{1,0:T(8,128)}, f32[512,512]{1,0:T(8,128)}, /*index=5*/f32[512,512]{1,0:...) custom-call(bf16[2,6144,256]{2,1,0:T(8,128)(2,1)} %get-tuple-element, ...), custom_call_target="tpu_custom_call" | custom-call | tf_op jit(solution)/shard_map/widen/pallas_call | solution.py:1307

commit v3 on v2

--- a/solution.py
+++ b/solution.py
@@ -32,33 +32,62 @@
 SMALL = 8
 LANES = D // 2
 CHUNKS = ((0, FF), (FF, FF), (ROW_OUT, 2 * D), (ROW_Q + D, 2 * D))
+DIMS = (("cyxab", "caxyb"), ("cxyq", "cyxq"), ("cyxq", "cxyq"), ("cyxq", "cxyq"))
 PARTS = 4
 LAYER_VMEM = 60 * 1024 * 1024
 WIDEN_VMEM = 60 * 1024 * 1024
 
 
-def both(*steps):
-    return tuple((chunk, color, k) for chunk, k in steps for color in range(2))
-
-
 ORDER = {
-    "down": both((0, 0)),
-    "up": both((0, 1), (1, 0)),
-    "branch": both((1, 1)),
-    "prepare": both(),
-    "near_a": both(),
-    "near_b": both((0, 2)),
-    "pair": both((1, 2)),
-    "far_0": both(),
-    "far_1": both((0, 3)),
-    "far_2": both((1, 3)),
-    "far_3": both(),
-    "query": both((2, 0)),
-    "state": both((2, 1), (0, 4)),
-    "close": both((1, 4)),
-    "key": both((3, 0)),
-    "back": both((0, 5), (2, 2), (3, 1)),
-    "tail": both((1, 5), (3, 2), (0, 6), (2, 3), (3, 3), (1, 6), (2, 4), (3, 4), (0, 7), (2, 5), (3, 5), (1, 7), (0, 8), (2, 6), (3, 6), (1, 8), (2, 7), (3, 7), (2, 8), (3, 8)),
+    "down": (
+        (0, 0, 0), (0, 1, 0),
+    ),
+    "up": (),
+    "branch": (),
+    "prepare": (
+        (1, 1, 0), (0, 1, 1), (1, 0, 0), (0, 0, 1),
+    ),
+    "near_a": (
+        (1, 0, 1), (1, 1, 1),
+    ),
+    "near_b": (
+        (0, 1, 2),
+    ),
+    "pair": (
+        (0, 0, 2),
+    ),
+    "far_0": (),
+    "far_1": (
+        (0, 1, 3), (1, 0, 2), (0, 0, 3), (1, 1, 2), (0, 1, 4),
+    ),
+    "far_2": (),
+    "far_3": (),
+    "query": (
+        (1, 0, 3),
+    ),
+    "state": (
+        (0, 0, 4),
+    ),
+    "close": (
+        (2, 1, 0), (2, 0, 0), (0, 1, 5),
+    ),
+    "key": (
+        (2, 1, 1), (3, 0, 0), (1, 1, 3), (3, 1, 0), (2, 0, 1), (3, 1, 1),
+        (1, 0, 4), (3, 0, 1), (2, 0, 2), (1, 1, 4), (2, 1, 2), (1, 0, 5),
+        (3, 0, 2), (2, 0, 3), (2, 1, 3), (3, 1, 2), (0, 1, 6), (1, 1, 5),
+        (0, 0, 5),
+    ),
+    "back": (
+        (1, 0, 6), (2, 0, 4), (2, 1, 4), (0, 0, 6), (3, 0, 3), (1, 1, 6),
+        (2, 0, 5), (0, 1, 7), (3, 1, 3), (2, 1, 5), (3, 0, 4), (0, 0, 7),
+        (3, 1, 4), (1, 0, 7), (1, 1, 7), (2, 0, 6),
+    ),
+    "tail": (
+        (0, 1, 8), (3, 0, 5), (3, 1, 5), (0, 0, 8), (2, 1, 6), (3, 0, 6),
+        (3, 1, 6), (2, 1, 7), (0, 1, 9), (2, 0, 7), (0, 0, 9), (3, 1, 7),
+        (1, 0, 8), (1, 1, 8), (3, 0, 7), (2, 0, 8), (2, 1, 8), (3, 1, 8),
+        (3, 0, 8), (0, 0, 10), (0, 1, 10),
+    ),
 }
 
 
@@ -132,21 +161,24 @@
     return size.bit_length() - 1
 
 
-def sum_order(color, n_rows, n_seq):
+def sum_order(dims, n_rows, n_seq):
     rows = [("rows", 2**b, 2) for b in range(bits(n_rows))]
     seq = [("seq", 2**b, 2) for b in range(bits(n_seq))]
-    last = []
-    if len(seq) > 2:
-        last = [("seq", seq[-2][1], 4)]
-        seq = seq[:-2]
-    if color == 0:
-        return rows + seq + last
-    return rows[:1] + seq + rows[1:] + last
-
-
-def sum_plan(color, n_rows, n_seq, rows, offset):
+    near, far = seq[:-2], seq[-2:]
+    found = {
+        "c": rows[:1],
+        "y": rows[1:],
+        "x": near,
+        "a": far[:1],
+        "b": far[1:],
+        "q": [("seq", far[0][1], 4)],
+    }
+    return [stage for dim in dims for stage in found[dim]]
+
+
+def sum_plan(dims, n_rows, n_seq, rows, offset):
     plan = []
-    for axis, low, group in sum_order(color, n_rows, n_seq):
+    for axis, low, group in sum_order(dims, n_rows, n_seq):
         steps = [(low, group)]
         if group == 4 and rows % 64:
             steps = [(low, 2), (2 * low, 2)]
@@ -162,10 +194,10 @@
 def sum_plans(n_rows, n_seq):
     plans = []
     offset = [0, 0]
-    for _base, rows in CHUNKS:
+    for (_base, rows), dims in zip(CHUNKS, DIMS):
         both = []
         for color in range(2):
-            plan, offset[color] = sum_plan(color, n_rows, n_seq, rows, offset[color])
+            plan, offset[color] = sum_plan(dims[color], n_rows, n_seq, rows, offset[color])
             both.append(plan)
         plans.append(both)
     return plans, max(offset)
@@ -423,7 +455,7 @@
         pay_s[0, u, 2 * E : PAY, :] = jnp.concatenate(norms, 0).astype(BF)
         return 0
 
-    lax.fori_loop(0, U, local_state, 0)
+    lax.fori_loop(0, U, local_state, 0, unroll=4)
 
     pl.semaphore_wait(barrier, jnp.minimum(sq, 2) + jnp.minimum(n - 1 - sq, 2) + len(greet))
 
@@ -598,23 +630,23 @@
             info_in[slot, 0] = jnp.full((8, T), -1.0, F32)
             info_in[slot, 1] = jnp.zeros((8, T), F32)
 
-    def half(which, r):
-        return pl.ds(which * HU + 2 * r, 2)
-
-    def chain_copy(way, stage, r):
+    def half(which, c):
+        return pl.ds(which * HU + c, 1)
+
+    def chain_copy(way, stage, c):
         step = 1 - 2 * way
-        here = pl.ds(2 * r, 2)
+        here = pl.ds(c, 1)
         src, dst, to = (
-            (pay_s.at[way, half(1 - par, r)], m1_r.at[way, here], partner),
+            (pay_s.at[way, half(1 - par, c)], m1_r.at[way, here], partner),
             (pass_s.at[way, here], carry_r.at[way, here], sq + 2 * step),
-            (give_s.at[way, here], in_s.at[way, half(par, r)], partner),
+            (give_s.at[way, here], in_s.at[way, half(par, c)], partner),
         )[stage]
-        return send(src, dst, chain_send.at[way, stage, r], chain_recv.at[way, stage, r], to)
-
-    def chain_arrival(way, stage, r):
-        here = pl.ds(2 * r, 2)
-        dst = (m1_r.at[way, here], carry_r.at[way, here], in_s.at[way, half(1 - par, r)])[stage]
-        return send(dst, dst, chain_send.at[way, stage, r], chain_recv.at[way, stage, r], partner)
+        return send(src, dst, chain_send.at[way, stage, c], chain_recv.at[way, stage, c], to)
+
+    def chain_arrival(way, stage, c):
+        here = pl.ds(c, 1)
+        dst = (m1_r.at[way, here], carry_r.at[way, here], in_s.at[way, half(1 - par, c)])[stage]
+        return send(dst, dst, chain_send.at[way, stage, c], chain_recv.at[way, stage, c], partner)
 
     def has_next(way):
         return (z + 1 < nz) if way == 0 else (z > 0)
@@ -635,8 +667,8 @@
         return inner, enter, through
 
     def chain_begin(way):
-        for r in range(R):
-            chain_copy(way, 0, r).start()
+        for c in range(HU):
+            chain_copy(way, 0, c).start()
 
         @pl.when(jnp.logical_not(has_before(way)))
         def _():
@@ -644,58 +676,54 @@
 
     def chain_pair(way):
         second = par == (1 - way)
-        for r in range(R):
-            chain_arrival(way, 0, r).wait_recv()
-            inner, enter, _through = marks(r)
+        for c in range(HU):
+            chain_arrival(way, 0, c).wait_recv()
+            inner, enter, _through = marks(c // 2)
             weight = inner if way == 0 else enter
             one = jnp.ones_like(weight)
             mine = jnp.where(second, one, weight)
             other = jnp.where(second, weight, one)
-            for j in range(2):
-                own = pay_s[way, par * HU + 2 * r + j].astype(F32)
-                got = m1_r[way, 2 * r + j].astype(F32)
-                sum_s[2 * r + j] = mine * own + other * got
+            own = pay_s[way, par * HU + c].astype(F32)
+            got = m1_r[way, c].astype(F32)
+            sum_s[c] = mine * own + other * got
 
     def chain_pass(way):
         second = par == (1 - way)
-        for r in range(R):
+        for c in range(HU):
 
             @pl.when(has_before(way))
             def _():
-                chain_arrival(way, 1, r).wait_recv()
-
-            inner, enter, through = marks(r)
+                chain_arrival(way, 1, c).wait_recv()
+
+            inner, enter, through = marks(c // 2)
             weight = enter if way == 0 else inner
-            for j in range(2):
-                carry = carry_r[way, 2 * r + j].astype(F32)
-                pass_s[way, 2 * r + j] = (sum_s[2 * r + j] + through * carry).astype(BF)
+            carry = carry_r[way, c].astype(F32)
+            pass_s[way, c] = (sum_s[c] + through * carry).astype(BF)
 
             @pl.when(has_next(way))
             def _():
-                chain_copy(way, 1, r).start()
-
-            for j in range(2):
-                carry = carry_r[way, 2 * r + j].astype(F32)
-                own = pay_s[way, par * HU + 2 * r + j].astype(F32)
-                got = m1_r[way, 2 * r + j].astype(F32)
-                later = jnp.where(second, got, own) + weight * carry
-                in_s[way, par * HU + 2 * r + j] = jnp.where(second, later, carry).astype(BF)
-                give_s[way, 2 * r + j] = jnp.where(second, carry, later).astype(BF)
-            chain_copy(way, 2, r).start()
+                chain_copy(way, 1, c).start()
+
+            own = pay_s[way, par * HU + c].astype(F32)
+            got = m1_r[way, c].astype(F32)
+            later = jnp.where(second, got, own) + weight * carry
+            in_s[way, par * HU + c] = jnp.where(second, later, carry).astype(BF)
+            give_s[way, c] = jnp.where(second, carry, later).astype(BF)
+            chain_copy(way, 2, c).start()
 
     def chain_finish(way):
-        for r in range(R):
-            chain_arrival(way, 2, r).wait_recv()
+        for c in range(HU):
+            chain_arrival(way, 2, c).wait_recv()
 
     def chain_drain(way):
-        for r in range(R):
-            chain_copy(way, 0, r).wait_send()
+        for c in range(HU):
+            chain_copy(way, 0, c).wait_send()
 
             @pl.when(has_next(way))
             def _():
-                chain_copy(way, 1, r).wait_send()
-
-            chain_copy(way, 2, r).wait_send()
+                chain_copy(way, 1, c).wait_send()
+
+            chain_copy(way, 2, c).wait_send()
 
     chain_begin(0)
 
@@ -731,7 +759,7 @@
             den_s[a, u] = nn(kernel, ones_pair)
         return 0
 
-    lax.fori_loop(0, U, far_local, 0)
+    lax.fori_loop(0, U, far_local, 0, unroll=4)
 
     for slot, step in enumerate((1, 2, -1)):
         came = (sq - step >= 0) & (sq - step < n)
@@ -781,10 +809,14 @@
         near_s[u, :HALO, :] += nn(ph_s[u].astype(BF), two_blocks(hv_s[u]))
         return 0
 
-    cut = z * U // nz
-    lax.fori_loop(0, cut, near_local, 0)
-    chain_pass(0)
-    lax.fori_loop(cut, U, near_local, 0)
+    entry = z * PARTS // nz
+    for part in range(PARTS):
+
+        @pl.when(entry == part)
+        def _():
+            chain_pass(0)
+
+        lax.fori_loop(part * U // PARTS, (part + 1) * U // PARTS, near_local, 0, unroll=3)
     chain_finish(0)
 
     def blend_lanes(a, u):
@@ -811,7 +843,7 @@
         mixed[rows, lanes] = blended.astype(BF)
         return 0
 
-    lax.fori_loop(0, U, far_finish, 0)
+    lax.fori_loop(0, U, far_finish, 0, unroll=4)
 
     loads[9].wait()
     middle[...] = tok[...].astype(F32) + nn(mixed[...], w_out[...])
@@ -842,9 +874,9 @@
         back_two[...] += nt(d_up, w_up[:, cols])
         return 0
 
-    lax.fori_loop(0, TILES // 2, feed, 0)
+    lax.fori_loop(0, TILES // 2, feed, 0, unroll=2)
     sums(ORDER["down"])
-    lax.fori_loop(TILES // 2, TILES, feed, 0)
+    lax.fori_loop(TILES // 2, TILES, feed, 0, unroll=2)
     sums(ORDER["up"])
     out[...] = (middle[...] + total[...]).astype(BF)
 
@@ -901,7 +933,7 @@
         pay_s[1, u, 2 * E : PAY, :] = jnp.concatenate(norms, 0).astype(BF)
         return 0
 
-    lax.fori_loop(0, U, far_prepare, 0)
+    lax.fori_loop(0, U, far_prepare, 0, unroll=4)
     chain_begin(1)
 
     def near_back(u, _):
@@ -934,9 +966,9 @@
         return 0
 
     sums(ORDER["prepare"])
-    lax.fori_loop(0, HU, near_back, 0)
+    lax.fori_loop(0, HU, near_back, 0, unroll=3)
     sums(ORDER["near_a"])
-    lax.fori_loop(HU, U, near_back, 0)
+    lax.fori_loop(HU, U, near_back, 0, unroll=3)
     sums(ORDER["near_b"])
 
     def halo_back(which, to):
@@ -993,7 +1025,7 @@
         def _():
             chain_pass(1)
 
-        lax.fori_loop(part * U // PARTS, (part + 1) * U // PARTS, far_back, 0)
+        lax.fori_loop(part * U // PARTS, (part + 1) * U // PARTS, far_back, 0, unroll=3)
         sums(ORDER["far_%d" % part])
 
     for u in range(U):
@@ -1033,7 +1065,7 @@
         wide_s[2, rows, lanes] = dv.astype(BF)
         return 0
 
-    lax.fori_loop(0, U, far_close, 0)
+    lax.fori_loop(0, U, far_close, 0, unroll=4)
     sums(ORDER["close"])
     for i in (1, 2):
         keep(ROW_Q + i * D, tn(normed[...], wide_s[i]))
@@ -1262,8 +1294,8 @@
             dma((3,)),
             dma((4,)),
             dma((4,)),
-            dma((2, 3, R)),
-            dma((2, 3, R)),
+            dma((2, 3, HU)),
+            dma((2, 3, HU)),
             dma((len(CHUNKS), 2, stages, 3)),
             dma((len(CHUNKS), 2, stages, 3)),
             dma((count,)),

time: 150 us -> 129 us (0.86)
  Pallas kernels: 149 us -> 128 us
    pallas_call x1, Pallas kernels: 141 us -> 119 us  [shards(): pl.pallas_call(functools.partial(layer_kernel, n, n_rows, R), out_shape=(...]
where the time goes in v3:
time: 129 us; the launch traced here: 128 us
  Pallas kernels  128 us (99%)
    pallas_call x1, Pallas kernels, shards(): pl.pallas_call(functools.partial(layer_kernel, n, n_rows, R), out_shape=(...  119 us
    pallas_call x1, Pallas kernels, shards(): pl.pallas_call(widen_kernel, out_shape=(jax.ShapeDtypeStruct((D,), F32),...  8.19 us

profile of v3, /device:TPU:1, one launch (start us, length us, event | category | flops | bytes accessed | tf_op | source)
XLA Modules:
  0.0 128.5 jit_solution(14491600672011265435)
XLA Ops:
  0.6 119.4 %layer.1 = (bf16[384,512]{1,0:T(8,128)(2,1)}, bf16[384,512]{1,0:T(8,128)(2,1)}, f32[8,512]{1,0:T(8,128)}, bf16[2,6144,256]{2,1,0:T(8,128)(2,1)}) custom-call(bf16[384,512]{1,0:T(8,128)(2,1)} %bitcast.6, s32[3,128]{1,0:T(4,128)} %seg_hbm.1, s32[3,128]{1,0:T(4,128)} %pad_hbm.1, f32[1,512]{1,0:T(1,128)} %bitcast.8, f32[1,512]{1,0:T(1,128)} %bitcast.9, ...), custom_call_target="tpu_custom_call" | custom-call | tf_op jit(solution)/shard_map/layer/pallas_call | solution.py:1305
  120.1 8.2 %widen.1 = (f32[512]{0:T(512)}, f32[512]{0:T(512)}, f32[2,8]{1,0:T(2,128)}, f32[512,512]{1,0:T(8,128)}, f32[512,512]{1,0:T(8,128)}, /*index=5*/f32[512,512]{1,0:...) custom-call(bf16[2,6144,256]{2,1,0:T(8,128)(2,1)} %get-tuple-element, ...), custom_call_target="tpu_custom_call" | custom-call | tf_op jit(solution)/shard_map/widen/pallas_call | solution.py:1339

commit v4 on v3

--- a/solution.py
+++ b/solution.py
@@ -409,13 +409,8 @@
         seg_row = seg[r : r + 1, :].astype(F32)
         pad_row = pad[r : r + 1, :].astype(F32)
         seg_j = jnp.broadcast_to(seg_row, (T, T))
-        pad_j = jnp.broadcast_to(pad_row, (T, T))
         seg_i = seg_j.T
-        pad_i = pad_j.T
-        same = seg_i == seg_j
-        open_key = same & (((j_pos < i_pos) & (pad_j == 1.0)) | (i_pos == j_pos))
-        far_mask[r] = open_key.astype(F32)
-        near_mask[r] = (open_key & (i_pos - j_pos <= BAND)).astype(F32)
+        pad_i = jnp.broadcast_to(pad_row, (T, T)).T
         last = seg_i[T - 1 : T, :]
         tail_mask[r] = ((seg_i == last) & (pad_i == 1.0)).astype(F32)
         use_mask[r] = seg_i
@@ -455,7 +450,10 @@
         pay_s[0, u, 2 * E : PAY, :] = jnp.concatenate(norms, 0).astype(BF)
         return 0
 
-    lax.fori_loop(0, U, local_state, 0, unroll=4)
+    def local_part(which):
+        return lambda i, _: local_state(which * HU + i, 0)
+
+    lax.fori_loop(0, HU, local_part(1 - par), 0, unroll=3)
 
     pl.semaphore_wait(barrier, jnp.minimum(sq, 2) + jnp.minimum(n - 1 - sq, 2) + len(greet))
 
@@ -726,12 +724,19 @@
             chain_copy(way, 2, c).wait_send()
 
     chain_begin(0)
+    lax.fori_loop(0, HU, local_part(par), 0, unroll=3)
 
     @pl.when(sq + 1 < n)
     def _():
         for which in range(2):
             halo_copy(which, sq + 1).start()
 
+    for r in range(R):
+        same = use_mask[r] == seg[r : r + 1, :].astype(F32)
+        pad_j = pad[r : r + 1, :]
+        open_key = same & (((j_pos < i_pos) & (pad_j == 1)) | (i_pos == j_pos))
+        far_mask[r] = open_key.astype(F32)
+        near_mask[r] = (open_key & (i_pos - j_pos <= BAND)).astype(F32)
     project(6, w_query, q_s)
     loads[7].wait()
     loads[8].wait()
@@ -933,8 +938,12 @@
         pay_s[1, u, 2 * E : PAY, :] = jnp.concatenate(norms, 0).astype(BF)
         return 0
 
-    lax.fori_loop(0, U, far_prepare, 0, unroll=4)
+    def prepare_part(which):
+        return lambda i, _: far_prepare(which * HU + i, 0)
+
+    lax.fori_loop(0, HU, prepare_part(1 - par), 0, unroll=3)
     chain_begin(1)
+    lax.fori_loop(0, HU, prepare_part(par), 0, unroll=3)
 
     def near_back(u, _):
         keys = two_blocks(k_s[u])
@@ -1067,8 +1076,11 @@
 
     lax.fori_loop(0, U, far_close, 0, unroll=4)
     sums(ORDER["close"])
-    for i in (1, 2):
-        keep(ROW_Q + i * D, tn(normed[...], wide_s[i]))
+    first = 2 - lax.rem(rw, 2)
+    keep(pl.multiple_of(ROW_Q + first * D, D), tn(normed[...], wide_s[first]))
+    sums(((3, 0, 0), (3, 1, 0)))
+    rest = 3 - first
+    keep(pl.multiple_of(ROW_Q + rest * D, D), tn(normed[...], wide_s[rest]))
     sums(ORDER["key"])
     for i, weight in ((1, w_key), (2, w_value)):
         back_two[...] += nt(wide_s[i], weight[...])
@@ -1130,7 +1142,7 @@
 
 def widen_kernel(
     grads,
-    small,
+    small_in,
     out_in,
     back_in,
     g_one,
@@ -1144,11 +1156,16 @@
     g_down,
     out,
     back,
+    small,
+    gains,
+    blends,
+    token,
     held,
     wide,
+    small_sem,
+    token_sem,
     in_sem,
     out_sem,
-    same_sem,
 ):
     blocks = ROWS_ALL // D
     targets = []
@@ -1156,36 +1173,50 @@
         targets += [g_down.at[pl.ds((t + i) * D, D)] for i in range(2)]
         targets += [g_up.at[:, pl.ds((t + i) * D, D)] for i in range(2)]
     targets += [g_out, g_query, g_key, g_value]
+    small_read = pltpu.make_async_copy(small_in, small, small_sem.at[0])
     reads = [
         pltpu.make_async_copy(grads.at[:, pl.ds(i * D, D)], held.at[i], in_sem.at[i])
         for i in range(blocks)
     ]
-    for read in reads:
+    token_reads = [
+        pltpu.make_async_copy(src, token.at[i], token_sem.at[i])
+        for i, src in enumerate((out_in, back_in))
+    ]
+    for read in [small_read] + reads + token_reads:
         read.start()
     writes = [
         pltpu.make_async_copy(wide.at[i], targets[i], out_sem.at[i]) for i in range(blocks)
     ]
-    same = [
-        pltpu.make_async_copy(out_in, out, same_sem.at[0]),
-        pltpu.make_async_copy(back_in, back, same_sem.at[1]),
+    small_writes = [
+        pltpu.make_async_copy(src, dst, small_sem.at[i + 1])
+        for i, (src, dst) in enumerate(
+            ((gains.at[0], g_one), (gains.at[1], g_two), (blends, g_blend))
+        )
     ]
-    for copy in same:
-        copy.start()
-    g_one[...] = small[0]
-    g_two[...] = small[1]
-    for a in range(2):
-        row = small[2 + a : 3 + a, :]
-        lane = lax.broadcasted_iota(jnp.int32, (H, D), 1) // E
-        head = lax.broadcasted_iota(jnp.int32, (H, D), 0)
-        per_head = jnp.sum(jnp.where(lane == head, row, 0.0), -1, keepdims=True)
-        g_blend[a : a + 1, :] = jnp.broadcast_to(per_head, (H, H)).T[:1]
+    token_writes = [
+        pltpu.make_async_copy(token.at[i], dst, token_sem.at[i + 2])
+        for i, dst in enumerate((out, back))
+    ]
     for i in range(blocks):
         reads[i].wait()
         wide[i, :, :LANES] = held[i, 0].astype(F32)
         wide[i, :, LANES:] = held[i, 1].astype(F32)
         writes[i].start()
-    for copy in writes + same:
-        copy.wait()
+    for read, write in zip(token_reads, token_writes):
+        read.wait()
+        write.start()
+    small_read.wait()
+    gains[...] = small[:2, :]
+    lane = lax.broadcasted_iota(jnp.int32, (H, D), 1) // E
+    head = lax.broadcasted_iota(jnp.int32, (H, D), 0)
+    for a in range(2):
+        row = small[2 + a : 3 + a, :]
+        per_head = jnp.sum(jnp.where(lane == head, row, 0.0), -1, keepdims=True)
+        blends[a : a + 1, :] = jnp.broadcast_to(per_head, (H, H)).T[:1]
+    for write in small_writes:
+        write.start()
+    for write in small_writes + writes + token_writes:
+        write.wait()
 
 
 def solution(mesh):
@@ -1351,14 +1382,19 @@
                 token,
                 token,
             ),
-            in_specs=[anyspace, vmem, vmem, vmem],
-            out_specs=(vmem,) * 3 + (anyspace,) * 8,
+            in_specs=[anyspace] * 4,
+            out_specs=(anyspace,) * 11,
             scratch_shapes=[
+                V((SMALL, D), F32),
+                V((2, D), F32),
+                V((2, H), F32),
+                V((2, M, D), BF),
                 V((blocks, 2, D, LANES), BF),
                 V((blocks, D, D), F32),
+                dma((4,)),
+                dma((4,)),
                 dma((blocks,)),
                 dma((blocks,)),
-                dma((2,)),
             ],
             compiler_params=pltpu.CompilerParams(vmem_limit_bytes=WIDEN_VMEM),
             name="widen",

time: 129 us -> 126 us (0.977)
  Pallas kernels: 128 us -> 125 us
    pallas_call x1, Pallas kernels: 8.19 us -> 6.78 us  [shards(): pl.pallas_call(widen_kernel, out_shape=(jax.ShapeDtypeStruct((D,), F32),...]
where the time goes in v4:
time: 126 us
  Pallas kernels  125 us (99%)
    pallas_call x1, Pallas kernels, shards(): pl.pallas_call(functools.partial(layer_kernel, n, n_rows, R), out_shape=(...  119 us
    pallas_call x1, Pallas kernels, shards(): pl.pallas_call(widen_kernel, out_shape=(jax.ShapeDtypeStruct((D,), F32),...  6.78 us

profile of v4, /device:TPU:1, one launch (start us, length us, event | category | flops | bytes accessed | tf_op | source)
XLA Modules:
  0.0 126.3 jit_solution(7598620449839852200)
XLA Ops:
  0.6 118.7 %layer.1 = (bf16[384,512]{1,0:T(8,128)(2,1)}, bf16[384,512]{1,0:T(8,128)(2,1)}, f32[8,512]{1,0:T(8,128)}, bf16[2,6144,256]{2,1,0:T(8,128)(2,1)}) custom-call(bf16[384,512]{1,0:T(8,128)(2,1)} %bitcast.6, s32[3,128]{1,0:T(4,128)} %seg_hbm.1, s32[3,128]{1,0:T(4,128)} %pad_hbm.1, f32[1,512]{1,0:T(1,128)} %bitcast.8, f32[1,512]{1,0:T(1,128)} %bitcast.9, ...), custom_call_target="tpu_custom_call" | custom-call | tf_op jit(solution)/shard_map/layer/pallas_call | solution.py:1336
  119.3 6.8 %widen.1 = (f32[512]{0:T(512)}, f32[512]{0:T(512)}, f32[2,8]{1,0:T(2,128)}, f32[512,512]{1,0:T(8,128)}, f32[512,512]{1,0:T(8,128)}, /*index=5*/f32[512,512]{1,0:...) custom-call(bf16[2,6144,256]{2,1,0:T(8,128)(2,1)} %get-tuple-element, ...), custom_call_target="tpu_custom_call" | custom-call | tf_op jit(solution)/shard_map/widen/pallas_call | solution.py:1370

commit v5 on v4

--- a/solution.py
+++ b/solution.py
@@ -353,7 +353,12 @@
     for both in plans:
         for plan in both:
             groups |= {(axis, low, group) for axis, low, group, *_ in plan}
-    greet = [(axis, low, group, d) for axis, low, group in sorted(groups) for d in range(1, group)]
+    greet = [
+        (axis, low, group, d)
+        for axis, low, group in sorted(groups)
+        for d in range(1, group)
+        if (axis, low) != ("seq", 1) and not (group == 2 and (axis, low, 4) in groups)
+    ]
     for axis, low, group, d in greet:
         pl.semaphore_signal(
             barrier, inc=1, device_id=peer_of(axis, low, group, d)[1], device_id_type=MESH
@@ -1081,7 +1086,7 @@
     sums(((3, 0, 0), (3, 1, 0)))
     rest = 3 - first
     keep(pl.multiple_of(ROW_Q + rest * D, D), tn(normed[...], wide_s[rest]))
-    sums(ORDER["key"])
+    sums(ORDER["key"][:8])
     for i, weight in ((1, w_key), (2, w_value)):
         back_two[...] += nt(wide_s[i], weight[...])
     gain_grad_one = jnp.zeros((1, D), F32)
@@ -1106,6 +1111,7 @@
         [gain_grad_one, gain_grad_two] + blends + [jnp.zeros((SMALL - 4, D), F32)], 0
     )
     small_step(0)
+    sums(ORDER["key"][8:])
     sums(ORDER["back"])
     for i, step in enumerate(ORDER["tail"]):
         sums((step,))

time: 126 us -> 126 us (level)
  no operation moved by 1% of the time
where the time goes in v5:
time: 126 us
  Pallas kernels  125 us (99%)
    pallas_call x1, Pallas kernels, shards(): pl.pallas_call(functools.partial(layer_kernel, n, n_rows, R), out_shape=(...  119 us
    pallas_call x1, Pallas kernels, shards(): pl.pallas_call(widen_kernel, out_shape=(jax.ShapeDtypeStruct((D,), F32),...  6.78 us

profile of v5, /device:TPU:1, one launch (start us, length us, event | category | flops | bytes accessed | tf_op | source)
XLA Modules:
  0.0 126.3 jit_solution(15680979340948199101)
XLA Ops:
  0.6 118.7 %layer.1 = (bf16[384,512]{1,0:T(8,128)(2,1)}, bf16[384,512]{1,0:T(8,128)(2,1)}, f32[8,512]{1,0:T(8,128)}, bf16[2,6144,256]{2,1,0:T(8,128)(2,1)}) custom-call(bf16[384,512]{1,0:T(8,128)(2,1)} %bitcast.6, s32[3,128]{1,0:T(4,128)} %seg_hbm.1, s32[3,128]{1,0:T(4,128)} %pad_hbm.1, f32[1,512]{1,0:T(1,128)} %bitcast.8, f32[1,512]{1,0:T(1,128)} %bitcast.9, ...), custom_call_target="tpu_custom_call" | custom-call | tf_op jit(solution)/shard_map/layer/pallas_call | solution.py:1342
  119.3 6.8 %widen.1 = (f32[512]{0:T(512)}, f32[512]{0:T(512)}, f32[2,8]{1,0:T(2,128)}, f32[512,512]{1,0:T(8,128)}, f32[512,512]{1,0:T(8,128)}, /*index=5*/f32[512,512]{1,0:...) custom-call(bf16[2,6144,256]{2,1,0:T(8,128)(2,1)} %get-tuple-element, ...), custom_call_target="tpu_custom_call" | custom-call | tf_op jit(solution)/shard_map/widen/pallas_call | solution.py:1376
